TPU v7x, 32 devices: a whole 2x2x4 slice. The times are simulated.
32 devices in a mesh: dp: 8 (over y, x, core), seq: 4 (over z).
Axes of the slice: x: 2, y: 2, z: 4, core: 2. Of those that a mesh axis runs over, the one named last changes fastest.
Arguments:
- tokens: bfloat16 [24, 2048, 768], P('dp', 'seq'), may hold values from -6 to 6
- w_qkv: bfloat16 [768, 2304], replicated, may hold values from -0.3125 to 0.3125
- w_out: bfloat16 [768, 768], replicated, may hold values from -0.875 to 0.875
- w_up: bfloat16 [768, 3072], replicated, may hold values from -0.21875 to 0.21875
- w_down: bfloat16 [3072, 768], replicated, may hold values from -0.109375 to 0.109375
- conv_filter: bfloat16 [33, 768], replicated, may hold values from -0.51953125 to 0.51953125
- gain_att: float32 [768], replicated, may hold values from 0.5 to 1.5
- gain_ffn: float32 [768], replicated, may hold values from 0.5 to 1.5
- grad_out: bfloat16 [24, 2048, 768], P('dp', 'seq'), may hold values from -6 to 6
Outputs:
- layer_out: bfloat16 [24, 2048, 768], P('dp', 'seq')
- grad_tokens: bfloat16 [24, 2048, 768], P('dp', 'seq')
- grad_w_qkv: float32 [768, 2304], P('dp', 'seq')
- grad_w_out: float32 [768, 768], P('dp', 'seq')
- grad_w_up: float32 [768, 3072], P('dp', 'seq')
- grad_w_down: float32 [3072, 768], P('dp', 'seq')
- grad_filter: float32 [33, 768], replicated
- grad_gain_att: float32 [768], replicated
- grad_gain_ffn: float32 [768], replicated
All inputs are finite; a program needn't handle non-finite values.
Results may differ from a plain program's by a relative error of at most 0.035.
Values may be sent and summed in bfloat16 or wider, within the bound.
A program may use at most 320 MiB of HBM per device.

v0:
```python
import jax
import jax.numpy as jnp
from jax import lax
from jax.sharding import PartitionSpec as P

H = 12
E = 64
M = 64
KW = 33
NEWTON = 6


highest = lax.Precision.HIGHEST
epsilon = 1e-05
root_half = 0.7071067811865476
inv_root_two_pi = 0.3989422804014327


def with_halo(cells, sides, width):
    for axis, dim in sides:
        count = lax.axis_size(axis)
        ends = count - 1
        head = lax.slice_in_dim(cells, 0, width, axis=dim)
        tail = lax.slice_in_dim(cells, cells.shape[dim] - width, cells.shape[dim], axis=dim)
        cells = jnp.concatenate(
            [
                lax.ppermute(tail, axis, [(i, (i + 1) % count) for i in range(ends)]),
                cells,
                lax.ppermute(head, axis, [((i + 1) % count, i) for i in range(ends)]),
            ],
            axis=dim,
        )
    return cells


def softmax_along(scores, axis):
    shifted = jnp.exp(scores - jnp.max(scores, axis=axis, keepdims=True))
    return shifted / jnp.sum(shifted, axis=axis, keepdims=True)


def norm_stats(residual):
    centre = residual - jnp.mean(residual, axis=-1, keepdims=True)
    row_scale = lax.rsqrt(jnp.mean(centre * centre, axis=-1, keepdims=True) + epsilon)
    return (centre * row_scale, row_scale)


def norm_back(grad_norm, normed, row_scale):
    return row_scale * (
        grad_norm
        - jnp.mean(grad_norm, axis=-1, keepdims=True)
        - normed * jnp.mean(grad_norm * normed, axis=-1, keepdims=True)
    )


def batch_product(left, right):
    return jnp.einsum("...ij,...jk->...ik", left, right, precision=highest)


def newton_inverse(kernel):
    column = jnp.sum(kernel, axis=-2)
    col_scale = 1.0 / jnp.max(column, axis=-1)
    approx = jnp.swapaxes(kernel, -1, -2) * col_scale[..., None, None]
    identity = jnp.eye(kernel.shape[-1], dtype=jnp.float32)
    for newton_step in range(NEWTON):
        product = batch_product(kernel, approx)
        inner_term = 7.0 * identity - product
        inner_term = 15.0 * identity - batch_product(product, inner_term)
        inner_term = 13.0 * identity - batch_product(product, inner_term)
        approx = 0.25 * batch_product(approx, inner_term)
    return approx


def landmark_mix(q_land, k_land, summary):
    middle = softmax_along(
        jnp.einsum("...mhe,...nhe->...hmn", q_land, k_land, precision=highest), -1
    )
    return batch_product(newton_inverse(middle), summary)


def depthwise(padded, taps, seq_len):
    result = jnp.zeros((padded.shape[0], seq_len, padded.shape[2]), jnp.float32)
    for tap_index in range(taps.shape[0]):
        result = result + taps[tap_index] * padded[:, tap_index : tap_index + seq_len]
    return result


def filter_grad(grad_mixed, padded, seq_len):
    per_tap = [
        jnp.einsum(
            "std,std->d",
            grad_mixed,
            padded[:, tap_index : tap_index + seq_len],
            preferred_element_type=jnp.float32,
        )
        for tap_index in range(KW)
    ]
    return jnp.stack(per_tap)


def per_device(tokens, w_qkv, w_out, w_up, w_down, conv_filter, gain_att, gain_ffn, grad_out):
    f32 = jnp.float32
    bf16 = jnp.bfloat16
    local_seqs, seq_len, features = tokens.shape
    seq_ranks = lax.axis_size("seq")
    seq_rank = lax.axis_index("seq")
    marks_here = M // seq_ranks
    seg_len = seq_len // marks_here
    rim_width = KW // 2
    row_count = local_seqs * seq_len
    flat_tokens = tokens.reshape(row_count, features)
    projected = jnp.dot(flat_tokens, w_qkv, preferred_element_type=f32)
    queries = (0.125 * projected[:, :features]).astype(bf16)
    key_rows = projected[:, features : 2 * features].astype(bf16)
    value_rows = projected[:, 2 * features :].astype(bf16)
    q_part = jnp.mean(
        queries.reshape(local_seqs, marks_here, seg_len, features), axis=2, dtype=f32
    ).astype(bf16)
    k_part = jnp.mean(
        key_rows.reshape(local_seqs, marks_here, seg_len, features), axis=2, dtype=f32
    ).astype(bf16)
    q_land, k_land = (
        lax.all_gather(q_part, "seq", axis=1, tiled=True),
        lax.all_gather(k_part, "seq", axis=1, tiled=True),
    )
    q_heads = queries.reshape(local_seqs, seq_len, H, E)
    k_heads = key_rows.reshape(local_seqs, seq_len, H, E)
    v_heads = value_rows.reshape(local_seqs, seq_len, H, E)
    ql_heads = q_land.reshape(local_seqs, M, H, E)
    kl_heads = k_land.reshape(local_seqs, M, H, E)
    first_probs = softmax_along(
        jnp.einsum("sthe,smhe->shmt", q_heads, kl_heads, preferred_element_type=f32), 2
    )
    first_low = first_probs.astype(bf16)
    third_scores = jnp.einsum("smhe,sthe->shmt", ql_heads, k_heads, preferred_element_type=f32)
    row_peak = lax.pmax(jnp.max(third_scores, axis=3), "seq")
    row_weights = jnp.exp(third_scores - row_peak[..., None])
    weights_low = row_weights.astype(bf16)
    row_total, numerator = (
        lax.psum(jnp.sum(row_weights, axis=3).astype(jnp.bfloat16), "seq").astype(jnp.float32),
        lax.psum(
            jnp.einsum("shmt,sthe->shme", weights_low, v_heads, preferred_element_type=f32).astype(
                jnp.bfloat16
            ),
            "seq",
        ).astype(jnp.float32),
    )
    summary = numerator / row_total[..., None]
    mixed_land, mix_pull = jax.vjp(
        landmark_mix, ql_heads.astype(f32), kl_heads.astype(f32), summary
    )
    mixed_low = mixed_land.astype(bf16)
    attended = jnp.einsum(
        "shmt,shme->sthe", first_low, mixed_low, preferred_element_type=f32
    ).reshape(local_seqs, seq_len, features)
    values_pad = with_halo(
        value_rows.reshape(local_seqs, seq_len, features), (("seq", 1),), rim_width
    )
    taps_wide = conv_filter.astype(f32)
    mixed_all = (attended + depthwise(values_pad, taps_wide, seq_len)).astype(bf16)
    mixed_flat = mixed_all.reshape(row_count, features)
    residual = flat_tokens.astype(f32) + jnp.dot(mixed_flat, w_out, preferred_element_type=f32)
    normed, scale_att = norm_stats(residual)
    hidden = normed * gain_att
    hidden_low = hidden.astype(bf16)
    up_proj = jnp.dot(hidden_low, w_up, preferred_element_type=f32)
    activated = (0.5 * up_proj * (1.0 + lax.erf(up_proj * root_half))).astype(bf16)
    residual_two = hidden + jnp.dot(activated, w_down, preferred_element_type=f32)
    normed_two, scale_ffn = norm_stats(residual_two)
    layer_out = (normed_two * gain_ffn).astype(bf16).reshape(local_seqs, seq_len, features)
    grad_top = grad_out.reshape(row_count, features).astype(f32)
    gain_ffn_grad = jnp.sum(grad_top * normed_two, axis=0)
    grad_resid_two = norm_back(grad_top * gain_ffn, normed_two, scale_ffn)
    grad_down_low = grad_resid_two.astype(bf16)
    down_grad = jnp.einsum("rf,rd->fd", activated, grad_down_low, preferred_element_type=f32)
    gelu_slope = (
        0.5 * (1.0 + lax.erf(up_proj * root_half))
        + up_proj * jnp.exp(-0.5 * up_proj * up_proj) * inv_root_two_pi
    )
    grad_up_low = (
        jnp.einsum("rd,fd->rf", grad_down_low, w_down, preferred_element_type=f32) * gelu_slope
    ).astype(bf16)
    up_grad = jnp.einsum("rd,rf->df", hidden_low, grad_up_low, preferred_element_type=f32)
    grad_hidden = grad_resid_two + jnp.einsum(
        "rf,df->rd", grad_up_low, w_up, preferred_element_type=f32
    )
    up_share, down_share = (
        lax.psum_scatter(
            up_grad.astype(jnp.bfloat16), "dp", scatter_dimension=0, tiled=True
        ).astype(jnp.float32),
        lax.psum_scatter(
            down_grad.astype(jnp.bfloat16), "dp", scatter_dimension=0, tiled=True
        ).astype(jnp.float32),
    )
    up_share, down_share = (
        lax.psum_scatter(
            up_share.astype(jnp.bfloat16), "seq", scatter_dimension=1, tiled=True
        ).astype(jnp.float32),
        lax.psum_scatter(
            down_share.astype(jnp.bfloat16), "seq", scatter_dimension=1, tiled=True
        ).astype(jnp.float32),
    )
    gain_att_grad = jnp.sum(grad_hidden * normed, axis=0)
    grad_resid = norm_back(grad_hidden * gain_att, normed, scale_att)
    grad_proj = grad_resid.astype(bf16)
    out_grad = jnp.einsum("rc,rd->cd", mixed_flat, grad_proj, preferred_element_type=f32)
    grad_mixed = (
        jnp.einsum("rd,cd->rc", grad_proj, w_out, preferred_element_type=f32)
        .astype(bf16)
        .reshape(local_seqs, seq_len, features)
    )
    grad_pad = with_halo(grad_mixed, (("seq", 1),), rim_width)
    taps_grad = filter_grad(grad_mixed, values_pad, seq_len)
    grad_conv_values = depthwise(grad_pad, taps_wide[::-1], seq_len)
    grad_heads = grad_mixed.reshape(local_seqs, seq_len, H, E)
    land_part = jnp.einsum("shmt,sthe->shme", first_low, grad_heads, preferred_element_type=f32)
    grad_first = jnp.einsum("sthe,shme->shmt", grad_heads, mixed_low, preferred_element_type=f32)
    grad_first_scores = (
        first_probs * (grad_first - jnp.sum(first_probs * grad_first, axis=2, keepdims=True))
    ).astype(bf16)
    grad_land = lax.psum(land_part.astype(jnp.bfloat16), "seq").astype(jnp.float32)
    mid_q, mid_k, grad_summary = mix_pull(grad_land)
    grad_summary_low = grad_summary.astype(bf16).astype(f32)
    grad_numer = (grad_summary_low / row_total[..., None]).astype(bf16)
    grad_total = -jnp.sum(grad_summary_low * summary, axis=3) / row_total
    grad_weights = (
        jnp.einsum("sthe,shme->shmt", v_heads, grad_numer, preferred_element_type=f32)
        + grad_total[..., None]
    )
    grad_third = (row_weights * grad_weights).astype(bf16)
    grad_values = (
        jnp.einsum("shmt,shme->sthe", weights_low, grad_numer, preferred_element_type=f32).reshape(
            local_seqs, seq_len, features
        )
        + grad_conv_values
    ).astype(bf16)
    q_land_part = jnp.einsum(
        "shmt,sthe->smhe", grad_third, k_heads, preferred_element_type=f32
    ).reshape(local_seqs, M, features)
    k_land_part = jnp.einsum(
        "shmt,sthe->smhe", grad_first_scores, q_heads, preferred_element_type=f32
    ).reshape(local_seqs, M, features)
    q_own, k_own = (
        lax.psum_scatter(
            q_land_part.astype(jnp.bfloat16), "seq", scatter_dimension=1, tiled=True
        ).astype(jnp.float32),
        lax.psum_scatter(
            k_land_part.astype(jnp.bfloat16), "seq", scatter_dimension=1, tiled=True
        ).astype(jnp.float32),
    )
    own_start = seq_rank * marks_here
    q_own = q_own + lax.dynamic_slice_in_dim(
        mid_q.reshape(local_seqs, M, features), own_start, marks_here, 1
    )
    k_own = k_own + lax.dynamic_slice_in_dim(
        mid_k.reshape(local_seqs, M, features), own_start, marks_here, 1
    )
    q_spread = jnp.broadcast_to(
        (q_own / seg_len)[:, :, None, :], (local_seqs, marks_here, seg_len, features)
    ).reshape(local_seqs, seq_len, features)
    k_spread = jnp.broadcast_to(
        (k_own / seg_len)[:, :, None, :], (local_seqs, marks_here, seg_len, features)
    ).reshape(local_seqs, seq_len, features)
    grad_queries = (
        jnp.einsum(
            "shmt,smhe->sthe", grad_first_scores, kl_heads, preferred_element_type=f32
        ).reshape(local_seqs, seq_len, features)
        + q_spread
    ).astype(bf16)
    grad_keys = (
        jnp.einsum("shmt,smhe->sthe", grad_third, ql_heads, preferred_element_type=f32).reshape(
            local_seqs, seq_len, features
        )
        + k_spread
    ).astype(bf16)
    grad_qkv = jnp.concatenate([grad_queries * 0.125, grad_keys, grad_values], axis=-1).reshape(
        row_count, 3 * features
    )
    qkv_grad = jnp.einsum("rc,rk->ck", flat_tokens, grad_qkv, preferred_element_type=f32)
    grad_tokens = (
        (grad_resid + jnp.einsum("rk,ck->rc", grad_qkv, w_qkv, preferred_element_type=f32))
        .astype(bf16)
        .reshape(local_seqs, seq_len, features)
    )
    qkv_share, out_share = (
        lax.psum_scatter(
            qkv_grad.astype(jnp.bfloat16), "dp", scatter_dimension=0, tiled=True
        ).astype(jnp.float32),
        lax.psum_scatter(
            out_grad.astype(jnp.bfloat16), "dp", scatter_dimension=0, tiled=True
        ).astype(jnp.float32),
    )
    qkv_share, out_share = (
        lax.psum_scatter(
            qkv_share.astype(jnp.bfloat16), "seq", scatter_dimension=1, tiled=True
        ).astype(jnp.float32),
        lax.psum_scatter(
            out_share.astype(jnp.bfloat16), "seq", scatter_dimension=1, tiled=True
        ).astype(jnp.float32),
    )
    taps_all, gain_att_all, gain_ffn_all = lax.psum(
        (taps_grad, gain_att_grad, gain_ffn_grad), ("dp", "seq")
    )
    return (
        layer_out,
        grad_tokens,
        qkv_share,
        out_share,
        up_share,
        down_share,
        taps_all,
        gain_att_all,
        gain_ffn_all,
    )


def solution(mesh):
    placed = (P("dp", "seq", None), P(), P(), P(), P(), P(), P(), P(), P("dp", "seq", None))
    return jax.shard_map(
        per_device,
        mesh=mesh,
        in_specs=placed,
        out_specs=(
            P("dp", "seq", None),
            P("dp", "seq", None),
            P("dp", "seq"),
            P("dp", "seq"),
            P("dp", "seq"),
            P("dp", "seq"),
            P(),
            P(),
            P(),
        ),
        check_vma=False,
    )
```

profile of v0, /device:TPU:0, one launch (start us, length us, event | category | flops | bytes accessed | tf_op | source)
XLA Modules:
  0.0 1147.1 jit_solution(12603610202142311780)
XLA Ops:
  9.2 7.4 fusion.254
  21.6 16.3 %all_gather.6 = bf16[3,64,768]{2,1,0:T(8,128)(2,1)} all-gather(bf16[3,16,768]{2,1,0:T(8,128)(2,1)S(1)} %multiply_convert_fusion.6), channel_id=1, replica_groups=mesh['dp'=8,'seq'=4] {'seq'}, dimensions={1}, use_global_device_ids=true | all-gather | bytes 368640 | tf_op jit(solution)/shard_map/all_gather | solution.py:122
  40.3 8.2 reshape.388
  48.5 7.3 copy.148
  55.8 5.4 fusion.256
  61.2 20.9 %pmax.7 = f32[3,12,64]{2,1,0:T(8,128)} all-reduce(f32[3,12,64]{2,1,0:T(8,128)} %get-tuple-element.127), channel_id=1, replica_groups=mesh['dp'=8,'seq'=4] {'seq'}, use_global_device_ids=true, to_apply=%region_7.0 | all-reduce | flops 2304 | bytes 18432 | tf_op jit(solution)/shard_map/pmax | solution.py:135
  82.2 8.2 reshape.389
  90.4 7.3 copy.150
  112.6 8.2 reshape.390
  123.1 17.4 %all_gather.7 = bf16[3,64,768]{2,1,0:T(8,128)(2,1)} all-gather(bf16[3,16,768]{2,1,0:T(8,128)(2,1)S(1)} %multiply_convert_fusion.5), channel_id=1, replica_groups=mesh['dp'=8,'seq'=4] {'seq'}, dimensions={1}, use_global_device_ids=true | all-gather | bytes 368640 | tf_op jit(solution)/shard_map/all_gather | solution.py:123
  196.9 7.3 copy.153
  204.2 6.1 fusion.257
  217.4 18.9 %psum.43 = bf16[3,12,64]{2,1,0:T(8,128)(2,1)S(1)} all-reduce(bf16[3,12,64]{2,1,0:T(8,128)(2,1)} %fusion.20), channel_id=1, replica_groups=mesh['dp'=8,'seq'=4] {'seq'}, use_global_device_ids=true, to_apply=%region_10.0 | all-reduce | flops 2304 | bytes 9216 | tf_op jit(solution)/shard_map/psum | solution.py:139
  250.6 5.6 fusion.179
  256.2 70.0 %fusion.11 = bf16[3,512,768]{1,2,0:T(8,128)(2,1)} fusion(f32[3,12,64,512]{3,2,1,0:T(8,128)} %fusion.179, bf16[3,512,768]{1,2,0:T(8,128)(2,1)} %copy.156, bf16[3,16,768]{1,2,0:T(8,128)(2,1)} %copy.159, bf16[3,16,768]{1,2,0:T(8,128)(2,1)} %copy.155, f32[768]{0:T(1024)} %get-tuple-element.74, f32[768]{0:T(1024)} %get-tuple-element.75, ...), kind=kLoop, calls=%fused_computation.83 | loop fusion | flops 231211008 | bytes 9686016 | tf_op jit(solution)/shard_map/convert_element_type | solution.py:159
  330.5 5.0 fusion.260
  336.2 17.6 %multiply_convert_fusion = (bf16[1536,3072]{1,0:T(8,128)(2,1)}, f32[1536,3072]{1,0:T(8,128)}) fusion(bf16[768,3072]{1,0:T(8,128)(2,1)} %param.12, f32[1536,768]{1,0:T(8,128)S(1)} %get-tuple-element.132, f32[768]{0:T(1024)S(1)} %copy-done.114, f32[1536]{0:T(1024)S(1)} %add_rsqrt_fusion.1, f32[1536]{0:T(1024)S(1)} %broadcast_multiply_fusion.5), kind=kOutput, calls=%fused_computation.8 | convolution fusion | flops 7276068864 | bytes 37764096 | tf_op jit(solution)/shard_map/dot_general | solution.py:165
  353.8 10.7 fusion.261
  371.5 19.4 %fusion.6 = bf16[1536,3072]{1,0:T(8,128)(2,1)} fusion(f32[1536,3072]{1,0:T(8,128)} %get-tuple-element.134, bf16[3072,768]{1,0:T(8,128)(2,1)S(1)} %bitcast.399, f32[1536,768]{1,0:T(8,128)S(1)} %get-tuple-element.116), kind=kOutput, calls=%fused_computation.7 | convolution fusion | flops 7296122880 | bytes 37748736 | tf_op jit(solution)/shard_map/rd,fd->rf/dot_general | solution.py:180
  390.9 15.2 %multiply_reduce_fusion.33 = (f32[768]{0:T(1024)}, f32[1536]{0:T(1024)S(1)}, f32[1536]{0:T(1024)S(1)}, f32[1536,768]{1,0:T(8,128)}) fusion(f32[1536,768]{1,0:T(8,128)S(1)} %get-tuple-element.132, f32[1536]{0:T(1024)S(1)} %add_rsqrt_fusion.1, f32[1536]{0:T(1024)S(1)} %broadcast_multiply_fusion.5, f32[768]{0:T(1024)S(1)} %copy-done.114, ...), kind=kOutput, calls=%fused_computation.129 | convolution fusion | flops 7258370048 | bytes 28342272 | tf_op jit(solution)/shard_map/rf,df->rd/dot_general | solution.py:183
  414.9 8.2 reshape.391
  423.1 7.4 copy.162
  435.3 6.9 multiply_reduce_fusion.34
  442.2 5.5 convolution_convert_fusion.3
  447.9 5.5 multiply_convert_fusion.2
  457.1 28.3 %all-reduce.7.cloned.1.call-done = bf16[3,12,64,64]{3,2,1,0:T(8,128)(2,1)} async-done(((bf16[3,12,64,64]{3,2,1,0:T(8,128)(2,1)}), bf16[3,12,64,64]{3,2,1,0:T(8,128)(2,1)}) %all-reduce.7.cloned.1.call-update) | async-done | bytes 294928 | tf_op jit(solution)/shard_map/psum | solution.py:220
  502.6 4.9 fusion.206
  639.7 69.5 %fusion.8 = bf16[3,512,768]{1,2,0:T(8,128)(2,1)} fusion(f32[3,12,64,512]{3,2,1,0:T(8,128)} %fusion.183, bf16[3,512,768]{1,2,0:T(8,128)(2,1)} %copy.200, bf16[3,16,768]{1,2,0:T(8,128)(2,1)} %copy.203, bf16[3,16,768]{1,2,0:T(8,128)(2,1)} %copy.199, f32[768]{0:T(1024)S(1)} %copy-done.92, f32[768]{0:T(1024)S(1)} %copy-done.93, f32[768]{0:T(1024)S(1)} %copy-done.94, ...), kind=kLoop, calls=%fused_computation.77 | loop fusion | flops 231211008 | bytes 9686016 | tf_op jit(solution)/shard_map/convert_element_type | solution.py:235
  712.7 6.1 copy.197
  718.8 6.0 fusion.9
  728.3 6.1 copy.191
  734.4 5.2 fusion.22
  741.1 11.5 %fusion.19 = bf16[768,2304]{0,1:T(8,128)(2,1)} fusion(bf16[3,512,768]{2,1,0:T(8,128)(2,1)S(1)} %copy-done.117, bf16[3,512,768]{1,2,0:T(8,128)(2,1)S(1)} %copy-done.60, bf16[3,512,768]{1,2,0:T(8,128)(2,1)S(1)} %copy-done.61, bf16[3,512,768]{1,2,0:T(8,128)(2,1)S(1)} %fusion.22), kind=kOutput, calls=%fused_computation.142 | convolution fusion | flops 5458821120 | bytes 12976128 | tf_op jit(solution)/shard_map/rc,rk->ck/dot_general | solution.py:278
  752.6 5.8 copy.435
  758.4 13.1 %convolution_convert_fusion = bf16[3072,768]{1,0:T(8,128)(2,1)} fusion(bf16[1536,3072]{1,0:T(8,128)(2,1)} %get-tuple-element.133, f32[1536,768]{1,0:T(8,128)} %copy-done.69), kind=kOutput, calls=%fused_computation.72 | convolution fusion | flops 7251296256 | bytes 18874368 | tf_op jit(solution)/shard_map/rf,rd->fd/dot_general | solution.py:174
  772.3 14.5 %convolution_convert_fusion.1 = bf16[768,3072]{1,0:T(8,128)(2,1)} fusion(bf16[1536,3072]{1,0:T(8,128)(2,1)} %fusion.6, f32[1536,768]{1,0:T(8,128)} %copy-done.31, f32[768]{0:T(1024)} %param.15, f32[1536]{0:T(1024)S(1)} %copy-done.98, f32[1536]{0:T(1024)S(1)} %copy-done.89), kind=kOutput, calls=%fused_computation.73 | convolution fusion | flops 7254835200 | bytes 18889728 | tf_op jit(solution)/shard_map/rd,rf->df/dot_general | solution.py:182
  793.3 21.7 %multiply_reduce_fusion.17 = (f32[768]{0:T(1024)S(1)}, f32[768]{0:T(1024)S(1)}, f32[768]{0:T(1024)S(1)}, f32[768]{0:T(1024)S(1)}, f32[768]{0:T(1024)}, /*index=5...) fusion(f32[768,3,512]{2,0,1:T(8,128)} %copy.241, bf16[3,512,768]{1,2,0:T(8,128)(2,1)} %copy.156, ...), kind=kLoop, calls=%fused_computation.113 | loop fusion | flops 74310912 | bytes 7179264 | tf_op jit(solution)/shard_map/std,std->d/dot_general | solution.py:89
  817.2 21.2 %multiply_reduce_fusion = (f32[768]{0:T(1024)S(1)}, f32[768]{0:T(1024)S(1)}, f32[768]{0:T(1024)S(1)}, f32[768]{0:T(1024)S(1)}, f32[768]{0:T(1024)S(1)}, /*index=...) fusion(f32[768,3,512]{2,0,1:T(8,128)} %copy.241, bf16[3,16,768]{1,2,0:T(8,128)(2,1)} %copy.159, ...), kind=kLoop, calls=%fused_computation.96 | loop fusion | flops 74310912 | bytes 7179264 | tf_op jit(solution)/shard_map/std,std->d/dot_general | solution.py:89
  849.0 16.6 %reduce-scatter.29.cloned.1.call-done = bf16[384,768]{1,0:T(8,128)(2,1)} async-done(((bf16[3072,768]{1,0:T(8,128)(2,1)}), bf16[384,768]{1,0:T(8,128)(2,1)}) %reduce-scatter.29.cloned.1.call-update) | async-done | bytes 589840 | tf_op jit(solution)/shard_map/reduce_scatter | solution.py:190
  867.8 16.9 %multiply_reduce_fusion.26 = (f32[768]{0:T(1024)S(1)}, f32[768]{0:T(1024)S(1)}, f32[768]{0:T(1024)S(1)}, f32[768]{0:T(1024)S(1)}, f32[768]{0:T(1024)S(1)}, /*index=5*/f32[768]{0:T(1024)S(1)}, f32[768]{0:T(1024)S(1)}) fusion(f32[768,3,512]{2,0,1:T(8,128)} %copy.241, bf16[3,512,768]{1,2,0:T(8,128)(2,1)} %copy.156, bf16[3,16,768]{1,2,0:T(8,128)(2,1)} %copy.155), kind=kLoop, calls=%fused_computation.122 | loop fusion | flops 57797376 | bytes 7173120 | tf_op jit(solution)/shard_map/std,std->d/dot_general | solution.py:89
  888.8 34.1 %reduce-scatter.25.cloned.1.call-done = bf16[96,3072]{1,0:T(8,128)(2,1)} async-done(((bf16[768,3072]{1,0:T(8,128)(2,1)}), bf16[96,3072]{1,0:T(8,128)(2,1)}) %reduce-scatter.25.cloned.1.call-update) | async-done | bytes 589840 | tf_op jit(solution)/shard_map/reduce_scatter | solution.py:187
  923.0 17.1 %multiply_reduce_fusion.9 = (f32[768]{0:T(1024)S(1)}, f32[768]{0:T(1024)S(1)}, f32[768]{0:T(1024)S(1)}, f32[768]{0:T(1024)S(1)}, f32[768]{0:T(1024)S(1)}, /*index=5*/f32[768]{0:T(1024)S(1)}, f32[768]{0:T(1024)S(1)}) fusion(f32[768,3,512]{2,0,1:T(8,128)} %copy.241, bf16[3,16,768]{1,2,0:T(8,128)(2,1)} %copy.159, bf16[3,512,768]{1,2,0:T(8,128)(2,1)} %copy.156), kind=kLoop, calls=%fused_computation.105 | loop fusion | flops 57797376 | bytes 7173120 | tf_op jit(solution)/shard_map/std,std->d/dot_general | solution.py:89
  945.7 6.8 stack.135
  952.5 40.0 %all-reduce = (f32[768]{0:T(1024)}, f32[768]{0:T(1024)}) all-reduce(f32[768]{0:T(1024)} %get-tuple-element.36, f32[768]{0:T(1024)S(1)} %copy-done.109), channel_id=1, replica_groups=mesh['dp'=8,'seq'=4] {'dp','seq'}, use_global_device_ids=true, to_apply=%region_41.0 | all-reduce | flops 1536 | bytes 12288 | tf_op jit(solution)/shard_map/psum | solution.py:300
  992.5 6.5 pad_maximum_fusion
  999.0 9.7 copy.204
  1008.7 10.6 add_convert_fusion
  1029.1 109.7 %all-reduce.9.cloned.1.call-done = f32[33,768]{1,0:T(8,128)} async-done(((f32[33,768]{1,0:T(8,128)}), f32[33,768]{1,0:T(8,128)}) %all-reduce.9.cloned.1.call-update) | async-done | bytes 101392 | tf_op jit(solution)/shard_map/psum | solution.py:300
  (485 shorter events, 332.9 us)
Async XLA Ops:
  7.2 240.5 %all-reduce.5.cloned.1.call-start = ((), (), s32[]{:S(2)}) async-start(), calls=%async_computation.10 | async-start | bytes 1179648 | tf_op jit(solution)/shard_map/psum | solution.py:140
  102.6 382.8 %all-reduce.7.cloned.1.call-start = ((), (), s32[]{:S(2)}) async-start(), calls=%async_computation.11 | async-start | bytes 1179648 | tf_op jit(solution)/shard_map/psum | solution.py:220
  104.2 139.6 %collective-permute-start = (bf16[3,16,768]{2,1,0:T(8,128)(2,1)}, bf16[3,16,768]{2,1,0:T(8,128)(2,1)}, u32[]{:S(2)}, u32[]{:S(2)}) collective-permute-start(bf16[3,16,768]{2,1,0:T(8,128)(2,1)} %get-tuple-element.120), channel_id=1, source_target_pairs={{0,1},{1,2},{2,3},{4,5},{5,6},{6,7},{8,9},{9,10},{10,11},{12,13},{... | collective-permute-start | bytes 221192 | tf_op jit(solution)/shard_map/ppermute | solution.py:27
  106.1 139.6 %collective-permute-start.1 = (bf16[3,16,768]{2,1,0:T(8,128)(2,1)}, bf16[3,16,768]{2,1,0:T(8,128)(2,1)}, u32[]{:S(2)}, u32[]{:S(2)}) collective-permute-start(bf16[3,16,768]{2,1,0:T(8,128)(2,1)} %get-tuple-element.121), channel_id=1, source_target_pairs={{1,0},{2,1},{3,2},{5,4},{6,5},{7,6},{9,8},{10,9},{11,10},{13,12},{... | collective-permute-start | bytes 221192 | tf_op jit(solution)/shard_map/ppermute | solution.py:29
  148.4 7.4 copy-start.100
  148.4 10.2 copy-start.115
  160.5 6.1 copy-start.58
  187.1 6.3 copy-start.20
  204.2 6.1 copy-start.95
  241.9 14.3 %copy-start.90 = (f32[768]{0:T(1024)}, f32[768]{0:T(1024)S(1)}, u32[]{:S(2)}) copy-start(f32[768]{0:T(1024)S(1)} %get-tuple-element.73) | copy-start | bytes 9220
  250.6 5.6 copy-start.119
  335.4 70.6 %copy-start.31 = (f32[1536,768]{1,0:T(8,128)}, f32[1536,768]{1,0:T(8,128)S(1)}, u32[]{:S(2)}) copy-start(f32[1536,768]{1,0:T(8,128)S(1)} %get-tuple-element.132) | copy-start | bytes 14155780
  335.4 70.6 %copy-start.88 = (f32[1536]{0:T(1024)}, f32[1536]{0:T(1024)S(1)}, u32[]{:S(2)}) copy-start(f32[1536]{0:T(1024)S(1)} %broadcast_multiply_fusion.5) | copy-start | bytes 18436
  335.5 18.4 %slice-start.2 = ((s8[4718592]{0:T(1024)(128)(4,1)}), s8[4194304]{0:T(1024)(128)(4,1)S(1)}, s32[]{:S(2)}) async-start(s8[4718592]{0:T(1024)(128)(4,1)} %bitcast.398), calls=%async_computation.25 | async-start | bytes 8388608
  336.2 69.9 %copy-start.97 = (f32[1536]{0:T(1024)}, f32[1536]{0:T(1024)S(1)}, u32[]{:S(2)}) copy-start(f32[1536]{0:T(1024)S(1)} %add_rsqrt_fusion.1) | copy-start | bytes 18436
  336.2 17.6 %slice-start.3 = ((s8[4718592]{0:T(1024)(128)(4,1)}), s8[524288]{0:T(1024)(128)(4,1)S(1)}, s32[]{:S(2)}) async-start(s8[4718592]{0:T(1024)(128)(4,1)} %bitcast.398), calls=%async_computation.26 | async-start | bytes 1048576
  371.5 19.4 %copy-start.69 = (f32[1536,768]{1,0:T(8,128)}, f32[1536,768]{1,0:T(8,128)S(1)}, u32[]{:S(2)}) copy-start(f32[1536,768]{1,0:T(8,128)S(1)} %get-tuple-element.116) | copy-start | bytes 14155780
  435.2 6.9 copy-start.71
  447.7 261.5 %reduce-scatter.19.cloned.1.call-start = ((), (), s32[]{:S(2)}) async-start(), calls=%async_computation.13 | async-start | bytes 368640 | tf_op jit(solution)/shard_map/reduce_scatter | solution.py:246
  447.9 5.5 copy-start.19
  457.1 267.7 %reduce-scatter.17.cloned.1.call-start = ((), (), s32[]{:S(2)}) async-start(), calls=%async_computation.12 | async-start | bytes 368640 | tf_op jit(solution)/shard_map/reduce_scatter | solution.py:243
  496.0 295.5 %reduce-scatter.23.cloned.1.call-start = ((), (), s32[]{:S(2)}) async-start(), calls=%async_computation.15 | async-start | bytes 1327104 | tf_op jit(solution)/shard_map/reduce_scatter | solution.py:288
  497.6 14.3 %collective-permute-start.2 = (bf16[3,16,768]{2,1,0:T(8,128)(2,1)}, bf16[3,16,768]{2,1,0:T(8,128)(2,1)}, u32[]{:S(2)}, u32[]{:S(2)}) collective-permute-start(bf16[3,16,768]{2,1,0:T(8,128)(2,1)} %get-tuple-element.118), channel_id=1, source_target_pairs={{0,1},{1,2},{2,3},{4,5},{5,6},{6,7},{8,9},{9,10},{10,11},{12,13},{... | collective-permute-start | bytes 221192 | tf_op jit(solution)/shard_map/ppermute | solution.py:27
  501.3 12.7 %collective-permute-start.3 = (bf16[3,16,768]{2,1,0:T(8,128)(2,1)}, bf16[3,16,768]{2,1,0:T(8,128)(2,1)}, u32[]{:S(2)}, u32[]{:S(2)}) collective-permute-start(bf16[3,16,768]{2,1,0:T(8,128)(2,1)} %get-tuple-element.119), channel_id=1, source_target_pairs={{1,0},{2,1},{3,2},{5,4},{6,5},{7,6},{9,8},{10,9},{11,10},{13,12},{... | collective-permute-start | bytes 221192 | tf_op jit(solution)/shard_map/ppermute | solution.py:29
  511.7 303.3 %reduce-scatter.31.cloned.1.call-start = ((), (), s32[]{:S(2)}) async-start(), calls=%async_computation.20 | async-start | bytes 3981312
  619.1 6.9 slice-start
  633.9 5.8 copy-start.91
  633.9 5.8 copy-start.92
  633.9 5.8 copy-start.93
  633.9 5.8 copy-start.94
  734.4 6.7 copy-start.60
  734.4 6.7 copy-start.61
  734.4 6.7 copy-start.117
  758.4 107.2 %reduce-scatter.29.cloned.1.call-start = ((), (), s32[]{:S(2)}) async-start(), calls=%async_computation.18 | async-start | bytes 5308416 | tf_op jit(solution)/shard_map/reduce_scatter | solution.py:190
  771.6 151.3 %reduce-scatter.25.cloned.1.call-start = ((), (), s32[]{:S(2)}) async-start(), calls=%async_computation.16 | async-start | bytes 5308416 | tf_op jit(solution)/shard_map/reduce_scatter | solution.py:187
  786.8 232.5 %reduce-scatter.33.cloned.1.call-start = ((), (), s32[]{:S(2)}) async-start(), calls=%async_computation.21 | async-start | bytes 245760
  793.2 229.0 %reduce-scatter.21.cloned.1.call-start = ((), (), s32[]{:S(2)}) async-start(), calls=%async_computation.14 | async-start | bytes 737280 | tf_op jit(solution)/shard_map/reduce_scatter | solution.py:293
  817.1 206.9 %reduce-scatter.35.cloned.1.call-start = ((), (), s32[]{:S(2)}) async-start(), calls=%async_computation.22 | async-start | bytes 737280
  817.1 21.2 %copy-start.108 = (f32[768]{0:T(1024)S(1)}, f32[768]{0:T(1024)}, u32[]{:S(2)}) copy-start(f32[768]{0:T(1024)} %get-tuple-element.62) | copy-start | bytes 9220
  817.2 21.8 %copy-start.107 = (f32[768]{0:T(1024)S(1)}, f32[768]{0:T(1024)}, u32[]{:S(2)}) copy-start(f32[768]{0:T(1024)} %get-tuple-element.61) | copy-start | bytes 9220
  817.2 22.4 %copy-start.106 = (f32[768]{0:T(1024)S(1)}, f32[768]{0:T(1024)}, u32[]{:S(2)}) copy-start(f32[768]{0:T(1024)} %get-tuple-element.60) | copy-start | bytes 9220
  817.2 23.0 %copy-start.105 = (f32[768]{0:T(1024)S(1)}, f32[768]{0:T(1024)}, u32[]{:S(2)}) copy-start(f32[768]{0:T(1024)} %get-tuple-element.59) | copy-start | bytes 9220
  817.2 23.5 %copy-start.104 = (f32[768]{0:T(1024)S(1)}, f32[768]{0:T(1024)}, u32[]{:S(2)}) copy-start(f32[768]{0:T(1024)} %get-tuple-element.58) | copy-start | bytes 9220
  867.7 159.7 %reduce-scatter.27.cloned.1.call-start = ((), (), s32[]{:S(2)}) async-start(), calls=%async_computation.17 | async-start | bytes 737280 | tf_op jit(solution)/shard_map/reduce_scatter | solution.py:195
  923.0 215.8 %all-reduce.9.cloned.1.call-start = ((), (), s32[]{:S(2)}) async-start(), calls=%async_computation.19 | async-start | bytes 245760 | tf_op jit(solution)/shard_map/psum | solution.py:300
  923.0 21.3 %copy-start.13 = (bf16[1536,768]{1,0:T(8,128)(2,1)S(1)}, bf16[1536,768]{1,0:T(8,128)(2,1)}, u32[]{:S(2)}) copy-start(bf16[1536,768]{1,0:T(8,128)(2,1)} %convolution_convert_fusion.2) | copy-start | bytes 7077892
  923.0 21.3 %copy-start.14 = (bf16[1536,768]{1,0:T(8,128)(2,1)S(1)}, bf16[1536,768]{1,0:T(8,128)(2,1)}, u32[]{:S(2)}) copy-start(bf16[1536,768]{1,0:T(8,128)(2,1)} %get-tuple-element.114) | copy-start | bytes 7077892
  944.3 8.2 copy-start.109
  (93 other events, 213.8 us)
Sparse Core Ops, SparseCore 0:
  102.7 39.3 all-reduce.4
  447.8 37.5 all-reduce.6
  488.2 20.4 reduce-scatter.18
  510.9 18.2 reduce-scatter.16
  532.2 35.0 reduce-scatter.22
  758.5 49.2 reduce-scatter.30
  811.7 53.8 reduce-scatter.28
  869.0 53.8 reduce-scatter.24
  925.9 19.3 reduce-scatter.32
  947.4 20.1 reduce-scatter.20
  969.9 20.3 reduce-scatter.34
  992.4 20.4 reduce-scatter.26
  1019.1 119.6 all-reduce.8
where the time goes:
time: 1160 us; the launch traced here: 1150 us
  matrix products  339 us (29%)
  other arithmetic  276 us (24%)
  local copies, waits for them, and re-layouts  204 us (18%)
  waiting for transfers between devices  189 us (16%)
  blocking collectives  114 us (10%)
  between operations  16.4 us (1%)
    dot_general x75, matrix products, batch_product(): return jnp.einsum('...ij,...jk->...ik', left, right, precision=highest)  149 us
    psum x1, waiting for transfers between devices, per_device(): lax.psum((taps_grad, gain_att_grad, gain_ffn_grad), ('dp', 'seq'))  110 us
    dot_general x5, other arithmetic, filter_grad(): jnp.einsum('std,std->d', grad_mixed, padded[:, tap_index:tap_index + seq_...  77.7 us
    convert_element_type x1, other arithmetic, per_device(): (attended + depthwise(values_pad, taps_wide, seq_len)).astype(bf16)  70 us
    convert_element_type x1, other arithmetic, per_device(): grad_values = (jnp.einsum('shmt,shme->sthe', weights_low, grad_numer, pre...  69.5 us
    psum x1, blocking collectives, per_device(): lax.psum((taps_grad, gain_att_grad, gain_ffn_grad), ('dp', 'seq'))  40 us
    unnamed x258, local copies, waits for them, and re-layouts  38.4 us
    reduce_scatter x1, waiting for transfers between devices, per_device(): lax.psum_scatter(up_grad.astype(jnp.bfloat16), 'dp', scatter_dimension=0,...  34.1 us
  transfers between devices with their start and end apart: 17, of which 4 were waited for; matrix products, arithmetic and copies ran while one was open for 48% of the time, Pallas kernels for 0%

commit v1 on v0

v1 whole, which is shorter than its diff:
```python
import functools

import jax
import jax.numpy as jnp
from jax import lax
from jax.experimental import pallas as pl
from jax.experimental.pallas import tpu as pltpu
from jax.sharding import PartitionSpec as P

H = 12
E = 64
M = 64
KW = 33
RIM = KW // 2
NEWTON = 6

f32 = jnp.float32
bf16 = jnp.bfloat16
epsilon = 1e-05
root_half = 0.7071067811865476
inv_root_two_pi = 0.3989422804014327
MB = 1 << 20

ERFC_P = 0.39
ERFC_C = (
    0.23532530842493793,
    0.09138785409700201,
    0.6495607954603394,
    -0.6354020079402325,
    0.8866654334206034,
    -0.22753738516480188,
)


def dot(a, b):
    return lax.dot_general(a, b, (((1,), (0,)), ((), ())), preferred_element_type=f32)


def dot_nt(a, b):
    return lax.dot_general(a, b, (((1,), (1,)), ((), ())), preferred_element_type=f32)


def dot_tn(a, b):
    return lax.dot_general(a, b, (((0,), (0,)), ((), ())), preferred_element_type=f32)


def lane_group(shape):
    return lax.broadcasted_iota(jnp.int32, shape, len(shape) - 1) // E


def group_masks(shape, count, dtype):
    groups = lane_group(shape)
    return [(groups == h).astype(f32).astype(dtype) for h in range(count)]


def block_diag(x, masks):
    return jnp.concatenate([x * m for m in masks], axis=0)


def diag_blocks(n, masks):
    return sum(n[E * h : E * h + E] * m for h, m in enumerate(masks))


def params(limit=None, **kw):
    return pltpu.CompilerParams(vmem_limit_bytes=limit, **kw)


def project_kernel(tok_ref, w_ref, q_ref, k_ref, v_ref, ql_ref, kl_ref):
    rows, features = tok_ref.shape[1:]
    marks = ql_ref.shape[1]
    seg = rows // marks
    x = tok_ref[0]
    row = lax.broadcasted_iota(jnp.int32, (marks, rows), 0)
    col = lax.broadcasted_iota(jnp.int32, (marks, rows), 1)
    mean = jnp.where(col // seg == row, 1.0 / seg, 0.0).astype(bf16)
    for part, out in enumerate((q_ref, k_ref, v_ref)):
        for c in range(0, features, 256):
            p = dot(x, w_ref[:, part * features + c : part * features + c + 256])
            if part == 0:
                p = 0.125 * p
            low = p.astype(bf16)
            out[0, :, c : c + 256] = low
            if part < 2:
                (ql_ref, kl_ref)[part][0, :, c : c + 256] = dot(mean, low).astype(bf16)


def project(tokens, w_qkv, marks):
    seqs, rows, features = tokens.shape
    full = pl.BlockSpec((1, rows, features), lambda s: (s, 0, 0))
    land = pl.BlockSpec((1, marks, features), lambda s: (s, 0, 0))
    return pl.pallas_call(
        project_kernel,
        grid=(seqs,),
        in_specs=[full, pl.BlockSpec(w_qkv.shape, lambda s: (0, 0))],
        out_specs=[full] * 3 + [land] * 2,
        out_shape=[jax.ShapeDtypeStruct(tokens.shape, bf16)] * 3
        + [jax.ShapeDtypeStruct((seqs, marks, features), bf16)] * 2,
        compiler_params=params(48 * MB),
        name="project",
    )(tokens, w_qkv)


def scores_kernel(q_ref, k_ref, v_ref, ql_ref, kl_ref, w_ref, p_ref, num_ref, stat_ref):
    rows, features = q_ref.shape[1:]
    masks = group_masks((M, 4 * E), 4, bf16)
    masks_wide = group_masks((M, 4 * E), 4, f32)
    ones = jnp.where(
        lane_group((4 * E, 4 * E)) == lax.broadcasted_iota(jnp.int32, (4 * E, 4 * E), 0) // E, 1.0, 0.0
    ).astype(bf16)
    stat_ref[...] = jnp.zeros_like(stat_ref)
    chunk = min(128, rows)
    upper = lax.broadcasted_iota(jnp.int32, (chunk, 2 * E), 1) >= E
    for g in range(features // 256):
        sl = slice(256 * g, 256 * g + 256)
        s3 = dot_nt(k_ref[0, :, sl], block_diag(ql_ref[0, :, sl], masks))
        peak = jnp.max(s3, axis=0, keepdims=True)
        e3 = jnp.exp(s3 - peak)
        total = jnp.sum(e3, axis=0, keepdims=True)
        low = e3.astype(bf16)
        w_ref[0, :, sl] = low
        num = diag_blocks(dot_tn(low, v_ref[0, :, sl]), masks_wide).astype(bf16)
        for i in range(2):
            lanes = slice(128 * i, 128 * i + 128)
            num_ref[2 * g + i] = num[:, lanes]
            stat_ref[2 * g + i, 0:1, :] = peak[:, lanes]
            stat_ref[2 * g + i, 1:2, :] = total[:, lanes]
        kd = block_diag(kl_ref[0, :, sl], masks)
        for r in range(0, rows, chunk):
            s1 = dot_nt(q_ref[0, r : r + chunk, sl], kd)
            parts = []
            for i in range(2):
                x = s1[:, 128 * i : 128 * i + 128]
                top_a = jnp.max(jnp.where(upper, -jnp.inf, x), axis=1, keepdims=True)
                top_b = jnp.max(jnp.where(upper, x, -jnp.inf), axis=1, keepdims=True)
                parts.append(jnp.exp(x - jnp.where(upper, top_b, top_a)))
            e1 = jnp.concatenate(parts, axis=1)
            p_ref[0, r : r + chunk, sl] = (e1 / dot(e1.astype(bf16), ones)).astype(bf16)


def scores(q, k, v, q_land, k_land):
    seqs, rows, features = q.shape
    pairs = features // 128
    full = pl.BlockSpec((1, rows, features), lambda s: (s, 0, 0))
    land = pl.BlockSpec((1, M, features), lambda s: (s, 0, 0))
    return pl.pallas_call(
        scores_kernel,
        grid=(seqs,),
        in_specs=[full] * 3 + [land] * 2,
        out_specs=[full] * 2
        + [
            pl.BlockSpec((pairs, M, 128), lambda s: (s, 0, 0)),
            pl.BlockSpec((pairs, 8, 128), lambda s: (s, 0, 0)),
        ],
        out_shape=[jax.ShapeDtypeStruct(q.shape, bf16)] * 2
        + [
            jax.ShapeDtypeStruct((seqs * pairs, M, 128), bf16),
            jax.ShapeDtypeStruct((seqs * pairs, 8, 128), f32),
        ],
        compiler_params=params(48 * MB),
        name="scores",
    )(q, k, v, q_land, k_land)


def fill_pad(pad, x_ref, l_ref, r_ref):
    rows = x_ref.shape[1]
    pad[0:RIM, :] = l_ref[0].astype(f32)
    pad[RIM : RIM + rows, :] = x_ref[0].astype(f32)
    pad[RIM + rows : RIM + rows + RIM, :] = r_ref[0].astype(f32)


def conv_kernel(v_ref, l_ref, r_ref, f_ref, o_ref, pad):
    rows = v_ref.shape[1]
    fill_pad(pad, v_ref, l_ref, r_ref)
    for c in range(0, rows, 64):
        acc = jnp.zeros((64, 128), f32)
        for j in range(KW):
            acc = acc + f_ref[j : j + 1, :] * pad[c + j : c + j + 64, :]
        o_ref[0, c : c + 64, :] = acc.astype(bf16)


def conv(v, left, right, taps):
    seqs, rows, features = v.shape
    sp = lambda n: pl.BlockSpec((1, n, 128), lambda s, g: (s, 0, g))
    return pl.pallas_call(
        conv_kernel,
        grid=(seqs, features // 128),
        in_specs=[sp(rows), sp(RIM), sp(RIM), pl.BlockSpec((KW, 128), lambda s, g: (0, g))],
        out_specs=sp(rows),
        out_shape=jax.ShapeDtypeStruct(v.shape, bf16),
        scratch_shapes=[pltpu.VMEM((rows + 2 * RIM, 128), f32)],
        name="conv",
    )(v, left, right, taps)


def conv_back_kernel(g_ref, l_ref, r_ref, v_ref, f_ref, o_ref, gf_ref, pad, facc):
    rows = v_ref.shape[1]
    fill_pad(pad, g_ref, l_ref, r_ref)

    @pl.when(pl.program_id(1) == 0)
    def _():
        facc[...] = jnp.zeros_like(facc)

    for c in range(0, rows, 64):
        acc = jnp.zeros((64, 128), f32)
        vals = v_ref[0, c : c + 64, :].astype(f32)
        for j in range(KW):
            moved = pad[c + 2 * RIM - j : c + 2 * RIM - j + 64, :]
            acc = acc + f_ref[j : j + 1, :] * moved
            facc[8 * j : 8 * j + 8, :] += (vals * moved).reshape(8, 8, 128).sum(0)
        o_ref[0, c : c + 64, :] = acc.astype(bf16)

    @pl.when(pl.program_id(1) == pl.num_programs(1) - 1)
    def _():
        gf_ref[...] = facc[...].reshape(KW, 8, 128).sum(1)


def conv_back(g, left, right, v, taps):
    seqs, rows, features = v.shape
    sp = lambda n: pl.BlockSpec((1, n, 128), lambda g, s: (s, 0, g))
    fs = pl.BlockSpec((KW, 128), lambda g, s: (0, g))
    return pl.pallas_call(
        conv_back_kernel,
        grid=(features // 128, seqs),
        in_specs=[sp(rows), sp(RIM), sp(RIM), sp(rows), fs],
        out_specs=[sp(rows), fs],
        out_shape=[jax.ShapeDtypeStruct(v.shape, bf16), jax.ShapeDtypeStruct((KW, features), f32)],
        scratch_shapes=[pltpu.VMEM((rows + 2 * RIM, 128), f32), pltpu.VMEM((KW * 8, 128), f32)],
        name="conv_back",
    )(g, left, right, v, taps)


def split(x):
    hi = x.astype(bf16)
    return hi, (x - hi.astype(f32)).astype(bf16)


def stack_parts(xs, axis):
    return jnp.concatenate([part for x in xs for part in split(x)], axis=axis)


def pair_sums(out, count):
    top = lambda i, j: out[128 * i + 64 * j : 128 * i + 64 * j + 64]
    return [
        top(i, 0)[:, :128] + (top(i, 0)[:, 128:] + top(i, 1)[:, :128]) for i in range(count)
    ]


def pair_nn(lefts, right, masks):
    hi, lo = split(right)
    packed = jnp.concatenate([block_diag(hi, masks), block_diag(lo, masks)], axis=1)
    return pair_sums(dot(stack_parts(lefts, 0), packed), len(lefts))


def pair_nt(lefts, right, masks):
    hi, lo = split(right)
    packed = jnp.concatenate([block_diag(hi, masks), block_diag(lo, masks)], axis=0)
    return pair_sums(dot_nt(stack_parts(lefts, 0), packed), len(lefts))


def pair_tn(left, rights, masks_wide):
    out = dot_tn(stack_parts([left], 1), stack_parts(rights, 1))
    results = []
    for i in range(len(rights)):
        full = out[:128, 256 * i : 256 * i + 128] + (
            out[:128, 256 * i + 128 : 256 * i + 256] + out[128:, 256 * i : 256 * i + 128]
        )
        results.append(diag_blocks(full, masks_wide))
    return results


def half_reduce(x, upper, op, fill):
    a = op(jnp.where(upper, fill, x), axis=1, keepdims=True)
    b = op(jnp.where(upper, x, fill), axis=1, keepdims=True)
    return jnp.where(upper, b, a)


def to_column(row, same, upper):
    return half_reduce(jnp.where(same, row, 0.0), upper, jnp.sum, 0.0)


def to_row(col, same):
    return jnp.sum(jnp.where(same, col, 0.0), axis=0, keepdims=True)


def pair_consts():
    lane = lax.broadcasted_iota(jnp.int32, (M, 128), 1)
    row = lax.broadcasted_iota(jnp.int32, (M, 128), 0)
    return lane >= E, row == lane % E, group_masks((M, 128), 2, bf16), group_masks((M, 128), 2, f32)


def inverse_kernel(
    num_ref, stat_ref, ql_ref, kl_ref, mixed_ref, sum_ref, mid_ref, z_ref, p_ref, a_ref, w_ref,
    scale_ref, tot_ref, alpha_ref,
):
    ranks, own = num_ref.shape[:2]
    upper, same, masks, masks_wide = pair_consts()
    for i in range(own):
        peak = stat_ref[0, i, 0:1, :]
        for r in range(1, ranks):
            peak = jnp.maximum(peak, stat_ref[r, i, 0:1, :])
        total = jnp.zeros((1, 128), f32)
        numer = jnp.zeros((M, 128), f32)
        for r in range(ranks):
            alpha = jnp.exp(stat_ref[r, i, 0:1, :] - peak)
            total = total + alpha * stat_ref[r, i, 1:2, :]
            column = to_column(alpha, same, upper)
            alpha_ref[r, i] = column
            numer = numer + column * num_ref[r, i].astype(f32)
        total = to_column(total, same, upper)
        tot_ref[i] = total
        sum_ref[i] = numer / total
        ql, kl = ql_ref[i], kl_ref[i]
        s2 = dot_nt(ql, block_diag(kl, masks))
        e2 = jnp.exp(s2 - half_reduce(s2, upper, jnp.max, -jnp.inf))
        middle = e2 / half_reduce(e2, upper, jnp.sum, 0.0)
        mid_ref[i] = middle
        st = dot_nt(kl, block_diag(ql, masks))
        et = jnp.exp(st - jnp.max(st, axis=0, keepdims=True))
        flipped = et / jnp.sum(et, axis=0, keepdims=True)
        column = jnp.sum(middle, axis=0, keepdims=True)
        scale = 1.0 / half_reduce(column, upper[0:1], jnp.max, -jnp.inf)
        scale_ref[i] = jnp.broadcast_to(scale, (8, 128))
        z_ref[0, i] = flipped * scale

    def step(it, carry):
        zs = [z_ref[it, i] for i in range(own)]
        ps = [pair_nn([mid_ref[i]], zs[i], masks)[0] for i in range(own)]
        second = [pair_nn([ps[i], zs[i]], ps[i], masks) for i in range(own)]
        for i in range(own):
            p2, a = second[i]
            w = 7.0 * ps[i] - p2
            p_ref[it, i] = ps[i]
            a_ref[it, i] = a
            w_ref[it, i] = w
            z_ref[it + 1, i] = 0.25 * (13.0 * zs[i] - 15.0 * a + pair_nn([a], w, masks)[0])
        return carry

    lax.fori_loop(0, NEWTON, step, 0)
    for i in range(own):
        mixed_ref[i] = pair_nn([z_ref[NEWTON, i]], sum_ref[i], masks)[0].astype(bf16)


def inverse(num, stat, ql, kl):
    ranks, own = num.shape[:2]
    mat = jax.ShapeDtypeStruct((own, M, 128), f32)
    steps = lambda n: jax.ShapeDtypeStruct((n, own, M, 128), f32)
    return pl.pallas_call(
        inverse_kernel,
        out_shape=[
            jax.ShapeDtypeStruct((own, M, 128), bf16), mat, mat, steps(NEWTON + 1), steps(NEWTON),
            steps(NEWTON), steps(NEWTON), jax.ShapeDtypeStruct((own, 8, 128), f32), mat, steps(ranks),
        ],
        compiler_params=params(48 * MB),
        name="inverse",
    )(num, stat, ql, kl)


def inverse_back_kernel(
    land_ref, ql_ref, kl_ref, sum_ref, mid_ref, z_ref, p_ref, a_ref, w_ref, scale_ref, tot_ref,
    alpha_ref, gn_ref, gt_ref, mq_ref, mk_ref, g_ref, dk_ref,
):
    ranks, own = land_ref.shape[:2]
    upper, same, masks, masks_wide = pair_consts()
    for i in range(own):
        land = land_ref[0, i].astype(f32)
        for r in range(1, ranks):
            land = land + land_ref[r, i].astype(f32)
        summary, total = sum_ref[i], tot_ref[i]
        gs = pair_tn(z_ref[NEWTON, i], [land], masks_wide)[0].astype(bf16).astype(f32)
        gn = (gs / total).astype(bf16).astype(f32)
        gt = -half_reduce(gs * summary, upper, jnp.sum, 0.0) / total
        for r in range(ranks):
            gn_ref[r, i] = (alpha_ref[r, i] * gn).astype(bf16)
            gt_ref[r, i] = jnp.broadcast_to(to_row(alpha_ref[r, i] * gt, same), (8, 128))
        g_ref[i] = pair_nt([land], summary, masks)[0]
        dk_ref[i] = jnp.zeros((M, 128), f32)

    def step(back, carry):
        it = NEWTON - 1 - back
        gs = [g_ref[i] for i in range(own)]
        das, dws = [], []
        for i in range(own):
            das.append(0.25 * (pair_nt([gs[i]], w_ref[it, i], masks)[0] - 15.0 * gs[i]))
            dws.append(0.25 * pair_tn(a_ref[it, i], [gs[i]], masks_wide)[0])
        dps, parts = [], []
        for i in range(own):
            right = pair_nt([dws[i], das[i]], p_ref[it, i], masks)
            left = pair_tn(p_ref[it, i], [dws[i]], masks_wide)[0]
            dps.append(7.0 * dws[i] - right[0] - left + pair_tn(z_ref[it, i], [das[i]], masks_wide)[0])
            parts.append(3.25 * gs[i] + right[1])
        for i in range(own):
            g_ref[i] = parts[i] + pair_tn(mid_ref[i], [dps[i]], masks_wide)[0]
            dk_ref[i] += pair_nt([dps[i]], z_ref[it, i], masks)[0]
        return carry

    lax.fori_loop(0, NEWTON, step, 0)
    eye = jnp.where(same, 1.0, 0.0).astype(bf16)
    for i in range(own):
        g, middle, scale = g_ref[i], mid_ref[i], scale_ref[i, 0:1, :]
        turned = dot_tn(stack_parts([g], 1), eye)
        turned = diag_blocks(turned[:128] + turned[128:], masks_wide)
        column = jnp.sum(middle, axis=0, keepdims=True)
        top = half_reduce(column, upper[0:1], jnp.max, -jnp.inf)
        hit = jnp.where(column == top, 1.0, 0.0)
        share = hit / half_reduce(hit, upper[0:1], jnp.sum, 0.0)
        d_scale = half_reduce(jnp.sum(turned * middle, axis=0, keepdims=True), upper[0:1], jnp.sum, 0.0)
        dk = dk_ref[i] + turned * scale - share * (d_scale * scale * scale)
        ds = middle * (dk - half_reduce(middle * dk, upper, jnp.sum, 0.0))
        hi, lo = split(ds)
        both = dot(jnp.concatenate([hi, lo], axis=0), block_diag(kl_ref[i], masks))
        mq_ref[i] = both[:M] + both[M:]
        turned = dot_tn(jnp.concatenate([hi, lo], axis=1), ql_ref[i])
        mk_ref[i] = diag_blocks(turned[:128] + turned[128:], masks_wide)


def inverse_back(land, ql, kl, saved):
    ranks, own = land.shape[:2]
    mat = jax.ShapeDtypeStruct((own, M, 128), f32)
    return pl.pallas_call(
        inverse_back_kernel,
        out_shape=[
            jax.ShapeDtypeStruct((ranks, own, M, 128), bf16),
            jax.ShapeDtypeStruct((ranks, own, 8, 128), f32), mat, mat,
        ],
        scratch_shapes=[pltpu.VMEM((own, M, 128), f32)] * 2,
        compiler_params=params(48 * MB),
        name="inverse_back",
    )(land, ql, kl, *saved)


def mean_of(x):
    return jnp.mean(x, axis=-1, keepdims=True)


def gelu_and_slope(u):
    x = jnp.abs(u) * root_half
    t = 1.0 / (1.0 + ERFC_P * x)
    poly = jnp.full_like(t, ERFC_C[-1])
    for c in ERFC_C[-2::-1]:
        poly = poly * t + c
    bell = jnp.exp(-0.5 * u * u)
    half = (0.5 * t) * poly * bell
    cdf = jnp.where(u < 0.0, half, 1.0 - half)
    return u * cdf, cdf + u * bell * inv_root_two_pi


def row_kernel(
    tok_ref, p_ref, conv_ref, mix_ref, top_ref, w_out_ref, w_up_ref, w_down_ref, ga_ref, gf_ref,
    out_ref, proj_ref, gm_ref, wg_ref, gains_ref,
    act, gul, slope, hid_t, gdl_t, mix_t, gpr, resid,
):
    step = pl.program_id(0)
    size, features = tok_ref.shape
    blocks = act.shape[0] // size
    ff = act.shape[1]
    wide = features

    @pl.when(step == 0)
    def _():
        gains_ref[...] = jnp.zeros_like(gains_ref)

    @pl.when(step < blocks)
    def _():
        start = pl.multiple_of(step * size, size)
        rows = pl.ds(start, size)
        masks = group_masks((M, 4 * E), 4, bf16)
        for g in range(features // 256):
            sl = slice(256 * g, 256 * g + 256)
            att = dot(p_ref[:, sl], block_diag(mix_ref[0, :, sl], masks))
            low = (att + conv_ref[:, sl].astype(f32)).astype(bf16)
            resid[:, sl] = low
        mixed = resid[...]
        mix_t[:, rows] = mixed.T
        residual = tok_ref[...].astype(f32) + dot(mixed, w_out_ref[...])
        centre = residual - mean_of(residual)
        s_att = lax.rsqrt(mean_of(centre * centre) + epsilon)
        normed = centre * s_att
        gain_att = ga_ref[...]
        hidden = normed * gain_att
        hid_low = hidden.astype(bf16)
        hid_t[:, rows] = hid_low.T
        down = jnp.zeros((size, features), f32)
        for j in range(0, ff, wide):
            up = dot(hid_low, w_up_ref[:, j : j + wide])
            a, sl = gelu_and_slope(up)
            low = a.astype(bf16)
            act[rows, j : j + wide] = low
            slope[:, j : j + wide] = sl.astype(bf16)
            down = down + dot(low, w_down_ref[j : j + wide, :])
        residual_two = hidden + down
        centre_two = residual_two - mean_of(residual_two)
        s_ffn = lax.rsqrt(mean_of(centre_two * centre_two) + epsilon)
        normed_two = centre_two * s_ffn
        gain_ffn = gf_ref[...]
        out_ref[...] = (normed_two * gain_ffn).astype(bf16)
        top = top_ref[...].astype(f32)
        gains_ref[8:16, :] += (top * normed_two).reshape(size // 8, 8, features).sum(0)
        g = top * gain_ffn
        grad_two = s_ffn * (g - mean_of(g) - normed_two * mean_of(g * normed_two))
        gdl = grad_two.astype(bf16)
        gdl_t[:, rows] = gdl.T
        back = jnp.zeros((size, features), f32)
        for j in range(0, ff, wide):
            gu = dot_nt(gdl, w_down_ref[j : j + wide, :]) * slope[:, j : j + wide].astype(f32)
            low = gu.astype(bf16)
            gul[rows, j : j + wide] = low
            back = back + dot_nt(low, w_up_ref[:, j : j + wide])
        grad_hidden = grad_two + back
        gains_ref[0:8, :] += (grad_hidden * normed).reshape(size // 8, 8, features).sum(0)
        g = grad_hidden * gain_att
        proj = (s_att * (g - mean_of(g) - normed * mean_of(g * normed))).astype(bf16)
        proj_ref[...] = proj
        gpr[rows, :] = proj
        gm_ref[...] = dot_nt(proj, w_out_ref[...]).astype(bf16)

    chunks = ff // wide
    for first, left, right in ((0, hid_t, gul), (chunks, gdl_t, act), (2 * chunks, mix_t, gpr)):
        count = chunks if first < 2 * chunks else 1

        @pl.when((step >= blocks + first) & (step < blocks + first + count))
        def _(first=first, left=left, right=right):
            base = (step - blocks - first) * wide
            for c in range(0, wide, 256):
                cols = pl.ds(pl.multiple_of(base + c, 256), 256)
                wg_ref[0, :, c : c + 256] = dot(left[...], right[:, cols]).astype(bf16)


def row_pass(tokens, probs, conv_out, mixed, grad_out, w_out, w_up, w_down, gain_att, gain_ffn):
    seqs, rows, features = tokens.shape
    ff = w_up.shape[1]
    size = min(256, rows)
    total = seqs * rows
    blocks = total // size
    grads = 2 * (ff // features) + 1
    here = lambda i: jnp.minimum(i, blocks - 1)
    block = pl.BlockSpec((size, features), lambda i: (here(i), 0))
    whole = lambda a: pl.BlockSpec(a.shape, lambda i: (0,) * a.ndim, pipeline_mode=pl.Buffered(1))
    flat = lambda a: a.reshape(total, features)
    gains = [gain_att.reshape(1, features), gain_ffn.reshape(1, features)]
    row_out = jax.ShapeDtypeStruct((total, features), bf16)
    tall = pltpu.VMEM((features, total), bf16)
    return pl.pallas_call(
        row_kernel,
        grid=(blocks + grads,),
        in_specs=[
            block, block, block,
            pl.BlockSpec((1, M, features), lambda i: (here(i) * size // rows, 0, 0)),
            block, whole(w_out), whole(w_up), whole(w_down), whole(gains[0]), whole(gains[1]),
        ],
        out_specs=[block] * 3
        + [
            pl.BlockSpec((1, features, features), lambda i: (jnp.maximum(i - blocks, 0), 0, 0)),
            pl.BlockSpec((16, features), lambda i: (0, 0)),
        ],
        out_shape=[row_out] * 3
        + [
            jax.ShapeDtypeStruct((grads, features, features), bf16),
            jax.ShapeDtypeStruct((16, features), f32),
        ],
        scratch_shapes=[
            pltpu.VMEM((total, ff), bf16), pltpu.VMEM((total, ff), bf16), pltpu.VMEM((size, ff), bf16),
            tall, tall, tall, pltpu.VMEM((total, features), bf16), pltpu.VMEM((size, features), bf16),
        ],
        compiler_params=params(60 * MB),
        name="row_pass",
    )(flat(tokens), flat(probs), flat(conv_out), mixed, flat(grad_out), w_out, w_up, w_down, *gains)


def first_back_kernel(gm_ref, p_ref, q_ref, mix_ref, kl_ref, land_ref, gq_ref, klp_ref):
    features = gm_ref.shape[2]
    masks = group_masks((M, 4 * E), 4, bf16)
    masks_wide = group_masks((M, 4 * E), 4, f32)
    ones = jnp.where(
        lane_group((4 * E, 4 * E)) == lax.broadcasted_iota(jnp.int32, (4 * E, 4 * E), 0) // E, 1.0, 0.0
    ).astype(bf16)
    for g in range(features // 256):
        sl = slice(256 * g, 256 * g + 256)
        gm, p = gm_ref[0, :, sl], p_ref[0, :, sl]
        land = diag_blocks(dot_tn(p, gm), masks_wide).astype(bf16)
        for i in range(2):
            land_ref[2 * g + i] = land[:, 128 * i : 128 * i + 128]
        d = dot_nt(gm, block_diag(mix_ref[0, :, sl], masks))
        pw = p.astype(f32)
        gs = (pw * (d - dot((pw * d).astype(bf16), ones))).astype(bf16)
        gq_ref[0, :, sl] = dot(gs, block_diag(kl_ref[0, :, sl], masks)).astype(bf16)
        klp_ref[0, :, sl] = diag_blocks(dot_tn(gs, q_ref[0, :, sl]), masks_wide)


def first_back(gm, probs, q, mixed, k_land):
    seqs, rows, features = q.shape
    pairs = features // 128
    full = pl.BlockSpec((1, rows, features), lambda s: (s, 0, 0))
    land = pl.BlockSpec((1, M, features), lambda s: (s, 0, 0))
    return pl.pallas_call(
        first_back_kernel,
        grid=(seqs,),
        in_specs=[full] * 3 + [land] * 2,
        out_specs=[pl.BlockSpec((pairs, M, 128), lambda s: (s, 0, 0)), full, land],
        out_shape=[
            jax.ShapeDtypeStruct((seqs * pairs, M, 128), bf16),
            jax.ShapeDtypeStruct(q.shape, bf16),
            jax.ShapeDtypeStruct((seqs, M, features), f32),
        ],
        compiler_params=params(48 * MB),
        name="first_back",
    )(gm, probs, q, mixed, k_land)


def third_back_kernel(w_ref, v_ref, k_ref, gc_ref, gn_ref, gt_ref, ql_ref, gv_ref, gk_ref, qlp_ref):
    features = w_ref.shape[2]
    masks = group_masks((M, 4 * E), 4, bf16)
    masks_wide = group_masks((M, 4 * E), 4, f32)
    for g in range(features // 256):
        sl = slice(256 * g, 256 * g + 256)
        w = w_ref[0, :, sl]
        gn = jnp.concatenate([gn_ref[2 * g], gn_ref[2 * g + 1]], axis=1)
        gt = jnp.concatenate([gt_ref[2 * g, 0:1, :], gt_ref[2 * g + 1, 0:1, :]], axis=1)
        gd = block_diag(gn, masks)
        gs = (w.astype(f32) * (dot_nt(v_ref[0, :, sl], gd) + gt)).astype(bf16)
        gv_ref[0, :, sl] = (dot(w, gd) + gc_ref[0, :, sl].astype(f32)).astype(bf16)
        gk_ref[0, :, sl] = dot(gs, block_diag(ql_ref[0, :, sl], masks)).astype(bf16)
        qlp_ref[0, :, sl] = diag_blocks(dot_tn(gs, k_ref[0, :, sl]), masks_wide)


def third_back(w, v, k, grad_conv, gn, gt, q_land):
    seqs, rows, features = v.shape
    pairs = features // 128
    full = pl.BlockSpec((1, rows, features), lambda s: (s, 0, 0))
    land = pl.BlockSpec((1, M, features), lambda s: (s, 0, 0))
    return pl.pallas_call(
        third_back_kernel,
        grid=(seqs,),
        in_specs=[full] * 4
        + [
            pl.BlockSpec((pairs, M, 128), lambda s: (s, 0, 0)),
            pl.BlockSpec((pairs, 8, 128), lambda s: (s, 0, 0)),
            land,
        ],
        out_specs=[full, full, land],
        out_shape=[jax.ShapeDtypeStruct(v.shape, bf16)] * 2
        + [jax.ShapeDtypeStruct((seqs, M, features), f32)],
        compiler_params=params(48 * MB),
        name="third_back",
    )(w, v, k, grad_conv, gn, gt, q_land)


def last_kernel(tok_ref, gq_ref, gk_ref, gv_ref, qo_ref, ko_ref, proj_ref, w_ref, gt_ref, wg_ref, d, tok_t):
    step = pl.program_id(0)
    seqs = tok_t.shape[1] // tok_ref.shape[1]
    rows, features = tok_ref.shape[1:]
    marks = qo_ref.shape[1]
    seg = rows // marks

    @pl.when(step < seqs)
    def _():
        here = pl.ds(pl.multiple_of(step * rows, rows), rows)
        for part, (core, own) in enumerate(((gq_ref, qo_ref), (gk_ref, ko_ref))):
            for m in range(marks):
                at = pl.ds(pl.multiple_of(step * rows + m * seg, seg), seg)
                x = core[0, m * seg : m * seg + seg, :].astype(f32) + own[0, m : m + 1, :] * (1.0 / seg)
                x = x.astype(bf16)
                if part == 0:
                    x = x * jnp.asarray(0.125, bf16)
                d[at, part * features : part * features + features] = x
        d[here, 2 * features :] = gv_ref[0]
        tok_t[:, here] = tok_ref[0].T
        for c in range(0, rows, 128):
            at = pl.ds(pl.multiple_of(step * rows + c, 128), 128)
            gt_ref[0, c : c + 128, :] = (
                proj_ref[0, c : c + 128, :].astype(f32) + dot_nt(d[at, :], w_ref[...])
            ).astype(bf16)

    @pl.when(step >= seqs)
    def _():
        base = (step - seqs) * features
        for c in range(0, features, 256):
            cols = pl.ds(pl.multiple_of(base + c, 256), 256)
            wg_ref[0, :, c : c + 256] = dot(tok_t[...], d[:, cols]).astype(bf16)


def last_pass(tokens, gq, gk, gv, q_own, k_own, proj, w_qkv):
    seqs, rows, features = tokens.shape
    marks = q_own.shape[1]
    here = lambda i: jnp.minimum(i, seqs - 1)
    full = pl.BlockSpec((1, rows, features), lambda i: (here(i), 0, 0))
    land = pl.BlockSpec((1, marks, features), lambda i: (here(i), 0, 0))
    return pl.pallas_call(
        last_kernel,
        grid=(seqs + 3,),
        in_specs=[full] * 4 + [land] * 2
        + [full, pl.BlockSpec(w_qkv.shape, lambda i: (0, 0), pipeline_mode=pl.Buffered(1))],
        out_specs=[full, pl.BlockSpec((1, features, features), lambda i: (jnp.maximum(i - seqs, 0), 0, 0))],
        out_shape=[
            jax.ShapeDtypeStruct(tokens.shape, bf16),
            jax.ShapeDtypeStruct((3, features, features), bf16),
        ],
        scratch_shapes=[
            pltpu.VMEM((seqs * rows, 3 * features), bf16), pltpu.VMEM((features, seqs * rows), bf16),
        ],
        compiler_params=params(56 * MB),
        name="last_pass",
    )(tokens, gq, gk, gv, q_own, k_own, proj, w_qkv)


def halo(cells, width):
    count = lax.axis_size("seq")
    head, tail = cells[:, :width], cells[:, cells.shape[1] - width :]
    left = lax.ppermute(tail, "seq", [(i, i + 1) for i in range(count - 1)])
    right = lax.ppermute(head, "seq", [(i + 1, i) for i in range(count - 1)])
    return left, right


def scatter_sum(grad):
    share = lax.psum_scatter(grad, "dp", scatter_dimension=0, tiled=True)
    return lax.psum_scatter(share, "seq", scatter_dimension=1, tiled=True).astype(f32)


def per_device(tokens, w_qkv, w_out, w_up, w_down, conv_filter, gain_att, gain_ffn, grad_out):
    seqs, rows, features = tokens.shape
    ranks = lax.axis_size("seq")
    rank = lax.axis_index("seq")
    marks = M // ranks
    ff = w_up.shape[1]
    pairs = seqs * (features // 128)
    own = -(-pairs // ranks)

    def to_pairs(x):
        x = x.reshape(seqs, M, features // 128, 128).transpose(0, 2, 1, 3)
        return x.reshape(pairs, M, 128)

    def from_pairs(x):
        x = x[:pairs].reshape(seqs, features // 128, M, 128).transpose(0, 2, 1, 3)
        return x.reshape(seqs, M, features)

    def pad_pairs(x):
        return jnp.pad(x, ((0, ranks * own - pairs),) + ((0, 0),) * (x.ndim - 1))

    def exchange(x):
        out = lax.all_to_all(pad_pairs(x), "seq", 0, 0, tiled=True)
        return out.reshape((ranks, own) + x.shape[1:])

    def mine(x):
        return lax.dynamic_slice_in_dim(pad_pairs(x), rank * own, own, 0)

    q, k, v, q_part, k_part = project(tokens, w_qkv, marks)
    land = lax.all_gather(jnp.stack([q_part, k_part]), "seq", axis=2, tiled=True)
    q_land, k_land = land[0], land[1]
    v_left, v_right = halo(v, RIM)
    taps = conv_filter.astype(f32)
    weights, probs, num, stat = scores(q, k, v, q_land, k_land)
    num_parts, stat_parts = exchange(num), exchange(stat)
    conv_out = conv(v, v_left, v_right, taps)
    ql_own, kl_own = mine(to_pairs(q_land)), mine(to_pairs(k_land))
    mixed_own, *saved = inverse(num_parts, stat_parts, ql_own, kl_own)
    mixed = from_pairs(lax.all_gather(mixed_own, "seq", axis=0, tiled=True))
    layer_out, proj, gm, wg, gains = row_pass(
        tokens, probs, conv_out, mixed, grad_out, w_out, w_up, w_down, gain_att, gain_ffn
    )
    shape3 = (seqs, rows, features)
    gm = gm.reshape(shape3)
    chunks = ff // features
    up_share = scatter_sum(wg[:chunks].transpose(1, 0, 2).reshape(features, ff))
    down_share = scatter_sum(wg[chunks : 2 * chunks].transpose(0, 2, 1).reshape(ff, features))
    out_share = scatter_sum(wg[2 * chunks])
    land_part, gq, k_land_part = first_back(gm, probs, q, mixed, k_land)
    g_left, g_right = halo(gm, RIM)
    land_parts = exchange(land_part)
    grad_conv, taps_grad = conv_back(gm, g_left, g_right, v, taps)
    gn_own, gt_own, mid_q, mid_k = inverse_back(land_parts, ql_own, kl_own, saved)

    def give_back(x):
        x = x.reshape((ranks * own,) + x.shape[2:])
        return lax.all_to_all(x, "seq", 0, 0, tiled=True)[:pairs]

    grad_values, gk, q_land_part = third_back(
        weights, v, k, grad_conv, give_back(gn_own), give_back(gt_own), q_land
    )

    def place(x):
        full = jnp.zeros((ranks * own, M, 128), f32)
        return from_pairs(lax.dynamic_update_slice_in_dim(full, x, rank * own, 0))

    both = jnp.stack([q_land_part + place(mid_q), k_land_part + place(mid_k)]).astype(bf16)
    both = both.reshape(2, seqs, ranks, marks, features).transpose(2, 0, 1, 3, 4)
    both = lax.all_to_all(both, "seq", 0, 0, tiled=True).astype(f32).sum(0)
    grad_tokens, qkv_grad = last_pass(tokens, gq, gk, grad_values, both[0], both[1], proj.reshape(shape3), w_qkv)
    qkv_share = scatter_sum(qkv_grad.transpose(1, 0, 2).reshape(features, 3 * features))
    gains = gains.reshape(2, 8, features).sum(1)
    small = lax.psum(jnp.concatenate([taps_grad, gains]), ("dp", "seq"))
    return (
        layer_out.reshape(shape3),
        grad_tokens,
        qkv_share,
        out_share,
        up_share,
        down_share,
        small[:KW],
        small[KW],
        small[KW + 1],
    )


def solution(mesh):
    placed = (P("dp", "seq", None), P(), P(), P(), P(), P(), P(), P(), P("dp", "seq", None))
    return jax.shard_map(
        per_device,
        mesh=mesh,
        in_specs=placed,
        out_specs=(
            P("dp", "seq", None),
            P("dp", "seq", None),
            P("dp", "seq"),
            P("dp", "seq"),
            P("dp", "seq"),
            P("dp", "seq"),
            P(),
            P(),
            P(),
        ),
        check_vma=False,
    )
```

time: 1160 us -> 627 us (0.54)
  matrix products: 339 us -> 0 us
  other arithmetic: 276 us -> 2.26 us
  Pallas kernels: 0 us -> 210 us
  local copies, waits for them, and re-layouts: 204 us -> 83.8 us
  blocking collectives: 114 us -> 46.9 us
  waiting for transfers between devices: 189 us -> 224 us
  starting transfers between devices: 9.02 us -> 33.9 us
    dot_general x101 -> x0, matrix products: 333 us -> none  [the longest x75 149 us: batch_product(): return jnp.einsum('...ij,...jk->...ik', left, right, precision=highest)]
    pallas_call x0 -> x10, Pallas kernels: none -> 210 us  [the longest x1 84 us: row_pass(): pl.pallas_call(row_kernel, grid=(blocks + grads,), in_specs=[block, block...]
    convert_element_type x11 -> x2, other arithmetic: 157 us -> 1.31 us  [the longest x1 0.66 us: per_device(): taps = conv_filter.astype(f32)]
    psum x3 -> x1, waiting for transfers between devices: 138 us -> 3.41 us  [per_device(): small = lax.psum(jnp.concatenate([taps_grad, gains]), ('dp', 'seq'))]
    unnamed x16 -> x13, waiting for transfers between devices: 0.22 us -> 106 us
    dot_general x5 -> x0, other arithmetic: 77.7 us -> none  [filter_grad(): jnp.einsum('std,std->d', grad_mixed, padded[:, tap_index:tap_index + seq_...]
    reshape x14 -> x4, local copies, waits for them, and re-layouts: 77.4 us -> 4.17 us  [the longest x1 2.06 us: from_pairs(): return x.reshape(seqs, M, features)]
    psum x2 -> x0, blocking collectives: 59 us -> none  [the longest x1 40 us: per_device(): lax.psum((taps_grad, gain_att_grad, gain_ffn_grad), ('dp', 'seq'))]
  transfers between devices with their start and end apart: 17 -> 18, of which waited for: 4 -> 12; matrix products, arithmetic and copies ran while one was open for 48% -> 10% of each run, Pallas kernels for 0% -> 14%
where the time goes in v1:
time: 627 us; the launch traced here: 617 us
  waiting for transfers between devices  224 us (36%)
  Pallas kernels  210 us (33%)
  local copies, waits for them, and re-layouts  83.8 us (13%)
  blocking collectives  46.9 us (7%)
  starting transfers between devices  33.9 us (5%)
  between operations  16.5 us (3%)
    unnamed x13, waiting for transfers between devices  106 us
    pallas_call x1, Pallas kernels, row_pass(): pl.pallas_call(row_kernel, grid=(blocks + grads,), in_specs=[block, block...  84 us
    reduce_scatter x2, waiting for transfers between devices, scatter_sum(): share = lax.psum_scatter(grad, 'dp', scatter_dimension=0, tiled=True)  55.6 us
    unnamed x72, local copies, waits for them, and re-layouts  44 us
    reduce_scatter x2, waiting for transfers between devices, scatter_sum(): lax.psum_scatter(share, 'seq', scatter_dimension=1, tiled=True).astype(f32)  43 us
    pallas_call x1, Pallas kernels, last_pass(): pl.pallas_call(last_kernel, grid=(seqs + 3,), in_specs=[full] * 4 + [land...  26.4 us
    pallas_call x1, Pallas kernels, conv_back(): pl.pallas_call(conv_back_kernel, grid=(features // 128, seqs), in_specs=[...  23.7 us
    all_gather x1, blocking collectives, per_device(): lax.all_gather(jnp.stack([q_part, k_part]), 'seq', axis=2, tiled=True)  18.2 us
  transfers between devices with their start and end apart: 18, of which 12 were waited for; matrix products, arithmetic and copies ran while one was open for 10% of the time, Pallas kernels for 14%

profile of v1, /device:TPU:0, one launch (start us, length us, event | category | flops | bytes accessed | tf_op | source)
XLA Modules:
  0.0 617.0 jit_solution(12092959707198632466)
XLA Ops:
  8.0 15.6 %project.1 = (bf16[3,512,768]{2,1,0:T(8,128)(2,1)S(1)}, bf16[3,512,768]{2,1,0:T(8,128)(2,1)S(1)}, bf16[3,512,768]{2,1,0:T(8,128)(2,1)}, bf16[3,16,768]{2,1,0:T(8,128)(2,1)S(1)}, bf16[3,16,768]{2,1,0:T(8,128)(2,1)S(1)}) custom-call(bf16[3,512,768]{2,1,0:T(8,128)(2,1)} %tok_ref.3, bf16[768,2304]{1,0:T(8,128)(2,1)} %w_ref.3), custom_call_target="tpu_custom_call" | custom-call | tf_op jit(solution)/shard_map/project/pallas_call | solution.py:91
  25.0 18.2 %all_gather.6 = bf16[2,3,64,768]{3,2,1,0:T(8,128)(2,1)S(1)} all-gather(bf16[2,3,16,768]{3,2,1,0:T(8,128)(2,1)S(1)} %pad_maximum_fusion.1), channel_id=1, replica_groups=mesh['dp'=8,'seq'=4] {'seq'}, dimensions={2}, use_global_device_ids=true | all-gather | bytes 737280 | tf_op jit(solution)/shard_map/all_gather | solution.py:746
  43.3 14.9 %scores.1 = (bf16[3,512,768]{2,1,0:T(8,128)(2,1)S(1)}, bf16[3,512,768]{2,1,0:T(8,128)(2,1)S(1)}, bf16[18,64,128]{2,1,0:T(8,128)(2,1)S(1)}, f32[18,8,128]{2,1,0:T(8,128)S(1)}) custom-call(bf16[3,512,768]{2,1,0:T(8,128)(2,1)} %copy-done.3, bf16[3,512,768]{2,1,0:T(8,128)(2,1)} %copy-done.2, bf16[3,512,768]{2,1,0:T(8,128)(2,1)} %get-tuple-element.49.v_ref, ...), custom_call_target="tpu_custom_call" | custom-call | tf_op jit(solution)/shard_map/scores/pallas_call | solution.py:145
  58.2 1.4 copy-done.1
  61.7 5.1 all-to-all-start.1
  67.6 5.0 all-to-all-done.1
  72.6 3.5 all-to-all-start
  77.0 3.9 collective-permute-start
  84.9 2.2 collective-permute-done.1.r_ref
  87.8 15.6 %conv.1 = bf16[3,512,768]{2,1,0:T(8,128)(2,1)} custom-call(bf16[3,512,768]{2,1,0:T(8,128)(2,1)} %get-tuple-element.49.v_ref, bf16[3,16,768]{2,1,0:T(8,128)(2,1)} %copy-done.24, bf16[3,16,768]{2,1,0:T(8,128)(2,1)} %copy-done.25, f32[33,768]{1,0:T(8,128)} %convert_element_type.27.f_ref), custom_call_target="tpu_custom_call" | custom-call | tf_op jit(solution)/shard_map/conv/pallas_call | solution.py:184
  103.3 5.4 inverse.1
  112.2 14.1 %all_gather.7 = bf16[20,64,128]{2,1,0:T(8,128)(2,1)S(1)} all-gather(bf16[5,64,128]{2,1,0:T(8,128)(2,1)S(1)} %get-tuple-element.55), channel_id=1, replica_groups=mesh['dp'=8,'seq'=4] {'seq'}, dimensions={0}, use_global_device_ids=true | all-gather | bytes 409600 | tf_op jit(solution)/shard_map/all_gather | solution.py:755
  127.3 2.1 reshape.111.mix_ref
  129.3 84.0 %row_pass.1 = (bf16[1536,768]{1,0:T(8,128)(2,1)}, bf16[1536,768]{1,0:T(8,128)(2,1)}, bf16[1536,768]{1,0:T(8,128)(2,1)}, bf16[9,768,768]{2,1,0:T(8,128)(2,1)}, f32[16,768]{1,0:T(8,128)}) custom-call(bf16[1536,768]{1,0:T(8,128)(2,1)} %bitcast.82, bf16[1536,768]{1,0:T(8,128)(2,1)} %bitcast.76, bf16[1536,768]{1,0:T(8,128)(2,1)} %bitcast.86, ...), custom_call_target="tpu_custom_call" | custom-call | tf_op jit(solution)/shard_map/row_pass/pallas_call | solution.py:542
  213.3 1.7 copy-done
  215.0 6.6 %first_back.1 = (bf16[18,64,128]{2,1,0:T(8,128)(2,1)S(1)}, bf16[3,512,768]{2,1,0:T(8,128)(2,1)S(1)}, f32[3,64,768]{2,1,0:T(8,128)S(1)}) custom-call(bf16[3,512,768]{2,1,0:T(8,128)(2,1)S(1)} %bitcast.75, bf16[3,512,768]{2,1,0:T(8,128)(2,1)} %copy-done.1, bf16[3,512,768]{2,1,0:T(8,128)(2,1)} %copy-done.3, bf16[3,64,768]{2,1,0:T(8,128)(2,1)S(1)} %copy-done.4, ...), custom_call_target="tpu_custom_call" | custom-call | tf_op jit(solution)/shard_map/first_back/pallas_call | solution.py:594
  224.6 4.1 all-to-all-start.2
  229.6 3.9 collective-permute-start.2
  238.3 11.9 %inverse_back.1 = (bf16[4,5,64,128]{3,2,1,0:T(8,128)(2,1)}, f32[4,5,8,128]{3,2,1,0:T(8,128)}, f32[5,64,128]{2,1,0:T(8,128)S(1)}, f32[5,64,128]{2,1,0:T(8,128)S(1)}) custom-call(bf16[4,5,64,128]{3,2,1,0:T(8,128)(2,1)S(1)} %bitcast.77, bf16[5,64,128]{2,1,0:T(8,128)(2,1)S(1)} %get-tuple-element.118.ql_ref, bf16[5,64,128]{2,1,0:T(8,128)(2,1)S(1)} %get-tuple-element.117.kl_ref, ...), custom_call_target="tpu_custom_call" | custom-call | tf_op jit(solution)/shard_map/inverse_back/pallas_call | solution.py:419
  251.5 5.2 all-to-all-start.4
  256.7 2.4 slice_bitcast_fusion.2
  259.9 23.7 %conv_back.1 = (bf16[3,512,768]{2,1,0:T(8,128)(2,1)}, f32[33,768]{1,0:T(8,128)}) custom-call(bf16[3,512,768]{2,1,0:T(8,128)(2,1)} %bitcast.74, bf16[3,16,768]{2,1,0:T(8,128)(2,1)} %copy-done.23, bf16[3,16,768]{2,1,0:T(8,128)(2,1)} %collective-permute-done.3.r_ref, bf16[3,512,768]{2,1,0:T(8,128)(2,1)} %get-tuple-element.49.v_ref, ...), custom_call_target="tpu_custom_call" | custom-call | tf_op jit(solution)/shard_map/conv_back/pallas_call | solution.py:221
  283.6 5.2 all-to-all-start.3
  289.2 6.9 %all-to-all-done.3 = bf16[20,64,128]{2,1,0:T(8,128)(2,1)S(1)} async-done(((bf16[20,64,128]{2,1,0:T(8,128)(2,1)}), bf16[20,64,128]{2,1,0:T(8,128)(2,1)S(1)}, u32[]{:S(2)}, u32[]{:S(2)}) %all-to-all-start.3) | async-done | bytes 327712 | tf_op jit(solution)/shard_map/all_to_all | solution.py:773
  296.1 5.9 third_back.1
  302.2 14.7 %all_to_all.30 = bf16[4,2,3,16,768]{4,3,2,1,0:T(8,128)(2,1)S(1)} all-to-all(bf16[4,2,3,16,768]{4,3,2,1,0:T(8,128)(2,1)S(1)} %copy_bitcast_fusion), channel_id=1, replica_groups=mesh['dp'=8,'seq'=4] {'seq'}, dimensions={0} | all-to-all | bytes 1179648 | tf_op jit(solution)/shard_map/all_to_all | solution.py:785
  317.7 26.4 %last_pass.1 = (bf16[3,512,768]{2,1,0:T(8,128)(2,1)}, bf16[3,768,768]{2,1,0:T(8,128)(2,1)}) custom-call(bf16[3,512,768]{2,1,0:T(8,128)(2,1)} %tok_ref.3, bf16[3,512,768]{2,1,0:T(8,128)(2,1)} %copy-done.6, bf16[3,512,768]{2,1,0:T(8,128)(2,1)} %copy-done.8, bf16[3,512,768]{2,1,0:T(8,128)(2,1)} %copy-done.7, f32[3,16,768]{2,1,0:T(8,128)} %get-tuple-element.116.qo_ref, ...), custom_call_target="tpu_custom_call" | custom-call | tf_op jit(solution)/shard_map/last_pass/pallas_call | solution.py:687
  344.1 4.3 copy.39
  348.4 4.0 copy.45
  352.5 8.1 %slice_bitcast_fusion = (bf16[4,768,768]{1,2,0:T(8,128)(2,1)}, bf16[768,4,768]{2,0,1:T(8,128)(2,1)}) fusion(bf16[9,768,768]{2,1,0:T(8,128)(2,1)} %get-tuple-element.82), kind=kLoop, calls=%fused_computation | loop fusion | bytes 18874368 | tf_op jit(solution)/shard_map/transpose | solution.py:763
  360.6 6.8 %copy.41 = bf16[4,768,768]{2,1,0:T(8,128)(2,1)} copy(bf16[4,768,768]{1,2,0:T(8,128)(2,1)} %get-tuple-element.105) | data formatting | bytes 9437184 | tf_op jit(solution)/shard_map/transpose | solution.py:763
  367.5 6.6 %copy.40 = bf16[768,4,768]{0,2,1:T(8,128)(2,1)} copy(bf16[768,4,768]{2,0,1:T(8,128)(2,1)} %get-tuple-element.106) | data formatting | bytes 9437184 | tf_op jit(solution)/shard_map/transpose | solution.py:762
  374.1 6.7 %copy.49 = bf16[768,3072]{1,0:T(8,128)(2,1)} copy(bf16[768,3072]{0,1:T(8,128)(2,1)} %bitcast.84) | data formatting | bytes 9437184
  382.5 1.7 copy.47
  384.3 15.3 %reduce-scatter.25.cloned.1.call-done = bf16[96,2304]{1,0:T(8,128)(2,1)} async-done(((bf16[768,2304]{1,0:T(8,128)(2,1)}), bf16[96,2304]{1,0:T(8,128)(2,1)}) %reduce-scatter.25.cloned.1.call-update) | async-done | bytes 442384
  399.6 2.1 copy.46
  401.7 55.6 %reduce-scatter.23.cloned.1.call-done = bf16[384,768]{1,0:T(8,128)(2,1)} async-done(((bf16[3072,768]{1,0:T(8,128)(2,1)}), bf16[384,768]{1,0:T(8,128)(2,1)}) %reduce-scatter.23.cloned.1.call-update) | async-done | bytes 589840 | tf_op jit(solution)/shard_map/reduce_scatter | solution.py:714
  457.3 2.1 copy.51
  459.5 55.1 %reduce-scatter.29.cloned.1.call-done = bf16[96,3072]{1,0:T(8,128)(2,1)} async-done(((bf16[768,3072]{1,0:T(8,128)(2,1)}), bf16[96,3072]{1,0:T(8,128)(2,1)}) %reduce-scatter.29.cloned.1.call-update) | async-done | bytes 589840
  514.6 2.2 copy.50
  516.9 3.4 all-reduce.7.cloned.1.call-done
  521.7 15.1 %reduce-scatter.27.cloned.1.call-done = bf16[192,96]{1,0:T(8,128)(2,1)} async-done(((bf16[768,96]{1,0:T(8,128)(2,1)}), bf16[192,96]{1,0:T(8,128)(2,1)}) %reduce-scatter.27.cloned.1.call-update) | async-done | bytes 36880
  538.4 20.8 %reduce-scatter.17.cloned.1.call-done = bf16[96,576]{0,1:T(8,128)(2,1)} async-done(((bf16[96,2304]{0,1:T(8,128)(2,1)}), bf16[96,576]{0,1:T(8,128)(2,1)}) %reduce-scatter.17.cloned.1.call-update) | async-done | bytes 110608 | tf_op jit(solution)/shard_map/reduce_scatter | solution.py:715
  559.1 1.7 copy.42
  560.9 20.8 %reduce-scatter.31.cloned.1.call-done = bf16[192,384]{1,0:T(8,128)(2,1)} async-done(((bf16[768,384]{1,0:T(8,128)(2,1)}), bf16[192,384]{1,0:T(8,128)(2,1)}) %reduce-scatter.31.cloned.1.call-update) | async-done | bytes 147472
  583.6 22.2 %reduce-scatter.21.cloned.1.call-done = bf16[96,768]{0,1:T(8,128)(2,1)} async-done(((bf16[96,3072]{0,1:T(8,128)(2,1)}), bf16[96,768]{0,1:T(8,128)(2,1)}) %reduce-scatter.21.cloned.1.call-update) | async-done | bytes 147472 | tf_op jit(solution)/shard_map/reduce_scatter | solution.py:715
  605.8 1.8 copy.43
  607.6 1.6 copy.65
  (122 shorter events, 33.0 us)
Async XLA Ops:
  23.6 1.4 copy-start.3
  25.0 18.3 %copy-start.2 = (bf16[3,512,768]{2,1,0:T(8,128)(2,1)}, bf16[3,512,768]{2,1,0:T(8,128)(2,1)S(1)}, u32[]{:S(2)}) copy-start(bf16[3,512,768]{2,1,0:T(8,128)(2,1)S(1)} %get-tuple-element.48.k_ref) | copy-start | bytes 7077892
  43.3 38.9 %copy-start.26 = (bf16[33,768]{1,0:T(8,128)(2,1)S(1)}, bf16[33,768]{1,0:T(8,128)(2,1)}, u32[]{:S(2)}) copy-start(bf16[33,768]{1,0:T(8,128)(2,1)} %param.14) | copy-start | bytes 152068
  58.2 1.4 copy-start.1
  59.6 1.4 copy-start.5
  61.7 22.0 %copy-start.28 = (f32[768]{0:T(1024)S(1)}, f32[768]{0:T(1024)}, u32[]{:S(2)}) copy-start(f32[768]{0:T(1024)} %param.15) | copy-start | bytes 9220
  61.7 22.6 %copy-start.29 = (f32[768]{0:T(1024)S(1)}, f32[768]{0:T(1024)}, u32[]{:S(2)}) copy-start(f32[768]{0:T(1024)} %param.16) | copy-start | bytes 9220
  61.7 10.9 %all-to-all-start.1 = ((f32[20,8,128]{2,1,0:T(8,128)}), f32[20,8,128]{2,1,0:T(8,128)S(1)}, u32[]{:S(2)}, u32[]{:S(2)}) async-start(f32[20,8,128]{2,1,0:T(8,128)} %pad.18), calls=%async_computation.1 | async-start | bytes 163840 | tf_op jit(solution)/shard_map/all_to_all | solution.py:739
  72.6 30.7 %all-to-all-start = ((bf16[20,64,128]{2,1,0:T(8,128)(2,1)}), bf16[20,64,128]{2,1,0:T(8,128)(2,1)S(1)}, u32[]{:S(2)}, u32[]{:S(2)}) async-start(bf16[20,64,128]{2,1,0:T(8,128)(2,1)} %pad.17), calls=%async_computation | async-start | bytes 655360 | tf_op jit(solution)/shard_map/all_to_all | solution.py:739
  77.0 7.9 %collective-permute-start = (bf16[3,16,768]{2,1,0:T(8,128)(2,1)S(1)}, bf16[3,16,768]{2,1,0:T(8,128)(2,1)S(1)}, u32[]{:S(2)}, u32[]{:S(2)}) collective-permute-start(bf16[3,16,768]{2,1,0:T(8,128)(2,1)S(1)} %get-tuple-element.110), channel_id=1, source_target_pairs={{0,1},{1,2},{2,3},{4,5},{5,6},{6,7},{8,9},{9,10},{10,11},{12,13},{... | collective-permute-start | bytes 221192 | tf_op jit(solution)/shard_map/ppermute | solution.py:708
  80.9 6.2 %collective-permute-start.1 = (bf16[3,16,768]{2,1,0:T(8,128)(2,1)S(1)}, bf16[3,16,768]{2,1,0:T(8,128)(2,1)S(1)}, u32[]{:S(2)}, u32[]{:S(2)}) collective-permute-start(bf16[3,16,768]{2,1,0:T(8,128)(2,1)S(1)} %get-tuple-element.109), channel_id=1, source_target_pairs={{1,0},{2,1},{3,2},{5,4},{6,5},{7,6},{9,8},{10,9},{11,10},{13,12},{... | collective-permute-start | bytes 221192 | tf_op jit(solution)/shard_map/ppermute | solution.py:709
  84.9 2.2 copy-start.24
  87.1 0.6 copy-start.25
  108.7 1.0 copy-start.9
  109.7 1.0 copy-start.10
  110.7 0.8 copy-start.12
  111.6 0.7 copy-start.16
  129.3 84.0 %copy-start.4 = (bf16[3,64,768]{2,1,0:T(8,128)(2,1)S(1)}, bf16[3,64,768]{2,1,0:T(8,128)(2,1)}, u32[]{:S(2)}) copy-start(bf16[3,64,768]{2,1,0:T(8,128)(2,1)} %reshape.111.mix_ref) | copy-start | bytes 884740
  213.3 1.7 copy-start
  215.0 21.0 %copy-start.17 = (f32[5,64,128]{2,1,0:T(8,128)S(1)}, f32[5,64,128]{2,1,0:T(8,128)}, u32[]{:S(2)}) copy-start(f32[5,64,128]{2,1,0:T(8,128)} %copy-done.16) | copy-start | bytes 491524
  221.6 1.4 copy-start.6
  223.0 0.8 copy-start.14
  224.6 11.5 %all-to-all-start.2 = ((bf16[20,64,128]{2,1,0:T(8,128)(2,1)}), bf16[20,64,128]{2,1,0:T(8,128)(2,1)S(1)}, u32[]{:S(2)}, u32[]{:S(2)}) async-start(bf16[20,64,128]{2,1,0:T(8,128)(2,1)} %pad.21), calls=%async_computation.2 | async-start | bytes 655360 | tf_op jit(solution)/shard_map/all_to_all | solution.py:739
  229.6 29.6 %collective-permute-start.2 = (bf16[3,16,768]{2,1,0:T(8,128)(2,1)S(1)}, bf16[3,16,768]{2,1,0:T(8,128)(2,1)S(1)}, u32[]{:S(2)}, u32[]{:S(2)}) collective-permute-start(bf16[3,16,768]{2,1,0:T(8,128)(2,1)S(1)} %get-tuple-element.108), channel_id=1, source_target_pairs={{0,1},{1,2},{2,3},{4,5},{5,6},{6,7},{8,9},{9,10},{10,11},{12,13},{... | collective-permute-start | bytes 221192 | tf_op jit(solution)/shard_map/ppermute | solution.py:708
  233.6 25.7 %collective-permute-start.3 = (bf16[3,16,768]{2,1,0:T(8,128)(2,1)S(1)}, bf16[3,16,768]{2,1,0:T(8,128)(2,1)}, u32[]{:S(2)}, u32[]{:S(2)}) collective-permute-start(bf16[3,16,768]{2,1,0:T(8,128)(2,1)S(1)} %get-tuple-element.107), channel_id=1, source_target_pairs={{1,0},{2,1},{3,2},{5,4},{6,5},{7,6},{9,8},{10,9},{11,10},{13,12},{... | collective-permute-start | bytes 221192 | tf_op jit(solution)/shard_map/ppermute | solution.py:709
  236.0 1.2 copy-start.11
  237.2 1.1 copy-start.13
  250.2 0.7 copy-start.18
  250.9 0.7 copy-start.20
  251.5 32.0 %all-to-all-start.4 = ((f32[20,8,128]{2,1,0:T(8,128)}), f32[20,8,128]{2,1,0:T(8,128)S(1)}, u32[]{:S(2)}, u32[]{:S(2)}) async-start(f32[20,8,128]{2,1,0:T(8,128)} %bitcast.26), calls=%async_computation.4 | async-start | bytes 163840 | tf_op jit(solution)/shard_map/all_to_all | solution.py:773
  256.7 125.7 %reduce-scatter.19.cloned.1.call-start = ((), (), s32[]{:S(2)}) async-start(), calls=%async_computation.15 | async-start | bytes 1327104 | tf_op jit(solution)/shard_map/reduce_scatter | solution.py:714
  259.2 29.7 %copy-start.21 = (f32[5,64,128]{2,1,0:T(8,128)S(1)}, f32[5,64,128]{2,1,0:T(8,128)}, u32[]{:S(2)}) copy-start(f32[5,64,128]{2,1,0:T(8,128)} %copy-done.20) | copy-start | bytes 491524
  259.2 0.6 copy-start.23
  283.6 5.4 copy-start.15
  283.6 5.5 copy-start.19
  283.6 12.5 %all-to-all-start.3 = ((bf16[20,64,128]{2,1,0:T(8,128)(2,1)}), bf16[20,64,128]{2,1,0:T(8,128)(2,1)S(1)}, u32[]{:S(2)}, u32[]{:S(2)}) async-start(bf16[20,64,128]{2,1,0:T(8,128)(2,1)} %bitcast.25), calls=%async_computation.3 | async-start | bytes 655360 | tf_op jit(solution)/shard_map/all_to_all | solution.py:773
  288.8 110.8 %reduce-scatter.25.cloned.1.call-start = ((), (), s32[]{:S(2)}) async-start(), calls=%async_computation.19 | async-start | bytes 3981312
  302.1 14.9 %copy-start.7 = (bf16[3,512,768]{2,1,0:T(8,128)(2,1)}, bf16[3,512,768]{2,1,0:T(8,128)(2,1)S(1)}, u32[]{:S(2)}) copy-start(bf16[3,512,768]{2,1,0:T(8,128)(2,1)S(1)} %get-tuple-element.74.gv_ref) | copy-start | bytes 7077892
  302.1 14.9 %copy-start.8 = (bf16[3,512,768]{2,1,0:T(8,128)(2,1)}, bf16[3,512,768]{2,1,0:T(8,128)(2,1)S(1)}, u32[]{:S(2)}) copy-start(bf16[3,512,768]{2,1,0:T(8,128)(2,1)S(1)} %get-tuple-element.73.gk_ref) | copy-start | bytes 7077892
  352.4 104.9 %reduce-scatter.23.cloned.1.call-start = ((), (), s32[]{:S(2)}) async-start(), calls=%async_computation.17 | async-start | bytes 5308416 | tf_op jit(solution)/shard_map/reduce_scatter | solution.py:714
  367.4 147.2 %reduce-scatter.29.cloned.1.call-start = ((), (), s32[]{:S(2)}) async-start(), calls=%async_computation.21 | async-start | bytes 5308416
  380.8 0.8 copy-start.27
  380.8 0.9 copy-start.22
  380.8 139.5 %all-reduce.7.cloned.1.call-start = ((), (), s32[]{:S(2)}) async-start(), calls=%async_computation.18 | async-start | bytes 245760 | tf_op jit(solution)/shard_map/psum | solution.py:789
  382.4 154.4 %reduce-scatter.27.cloned.1.call-start = ((), (), s32[]{:S(2)}) async-start(), calls=%async_computation.20 | async-start | bytes 245760
  384.2 174.9 %reduce-scatter.17.cloned.1.call-start = ((), (), s32[]{:S(2)}) async-start(), calls=%async_computation.14 | async-start | bytes 737280 | tf_op jit(solution)/shard_map/reduce_scatter | solution.py:715
  401.7 180.0 %reduce-scatter.31.cloned.1.call-start = ((), (), s32[]{:S(2)}) async-start(), calls=%async_computation.22 | async-start | bytes 737280
  459.5 146.3 %reduce-scatter.21.cloned.1.call-start = ((), (), s32[]{:S(2)}) async-start(), calls=%async_computation.16 | async-start | bytes 983040 | tf_op jit(solution)/shard_map/reduce_scatter | solution.py:715
Sparse Core Ops, SparseCore 0:
  260.8 38.2 reduce-scatter.18
  352.5 46.9 reduce-scatter.24
  403.4 53.8 reduce-scatter.22
  460.6 53.9 reduce-scatter.28
  517.4 19.3 reduce-scatter.26
  538.9 20.1 reduce-scatter.16
  561.4 20.2 reduce-scatter.30
  584.0 21.7 reduce-scatter.20
Sparse Core Ops, SparseCore 1:
  387.4 132.8 all-reduce.6

commit v2 on v1

--- a/solution.py
+++ b/solution.py
@@ -65,10 +65,82 @@
     return pltpu.CompilerParams(vmem_limit_bytes=limit, **kw)
 
 
-def project_kernel(tok_ref, w_ref, q_ref, k_ref, v_ref, ql_ref, kl_ref):
+MESH = pl.DeviceIdType.MESH
+ANY = pl.BlockSpec(memory_space=pl.ANY)
+
+
+def seq_place():
+    return lax.axis_index("seq"), lax.axis_size("seq")
+
+
+def seq_peers():
+    me, count = seq_place()
+    return [(o, lax.rem(me + o, count)) for o in range(1, count)]
+
+
+def greet(extra=()):
+    barrier = pltpu.get_barrier_semaphore()
+    targets = [{"seq": peer} for _, peer in seq_peers()] + list(extra)
+    for target in targets:
+        pl.semaphore_signal(barrier, inc=1, device_id=target, device_id_type=MESH)
+    pl.semaphore_wait(barrier, len(targets))
+
+
+def remote(src, dst, send, recv, target):
+    return pltpu.make_async_remote_copy(
+        src_ref=src, dst_ref=dst, send_sem=send, recv_sem=recv, device_id=target, device_id_type=MESH
+    )
+
+
+def swap_copies(src, dst, own, sems):
+    me, count = seq_place()
+    copies = [
+        remote(src.at[pl.ds(peer * own, own)], dst.at[me], sems.at[0, o], sems.at[1, o], {"seq": peer})
+        for o, peer in seq_peers()
+    ]
+    return copies, pltpu.make_async_copy(src.at[pl.ds(me * own, own)], dst.at[me], sems.at[0, 0])
+
+
+def spread_copies(src, dst, own, sems):
+    me, count = seq_place()
+    at = dst.at[pl.ds(me * own, own)]
+    copies = [
+        remote(src, at, sems.at[0, o], sems.at[1, o], {"seq": peer}) for o, peer in seq_peers()
+    ]
+    return copies, pltpu.make_async_copy(src, at, sems.at[0, 0])
+
+
+def begin(pair):
+    for copy in pair[0]:
+        copy.start()
+    pair[1].start()
+
+
+def finish(pair):
+    for copy in pair[0]:
+        copy.wait()
+    pair[1].wait()
+
+
+def rank_sems():
+    return pltpu.SemaphoreType.DMA((2, lax.axis_size("seq")))
+
+
+def project_kernel(
+    tok_ref, w_ref, q_ref, k_ref, v_ref, land_out, rim_out, land, rim, send, recv, local, rim_send, rim_recv,
+    rim_local,
+):
+    step = pl.program_id(0)
+    seqs = pl.num_programs(0)
+    me, count = seq_place()
     rows, features = tok_ref.shape[1:]
-    marks = ql_ref.shape[1]
+    marks = land.shape[2]
     seg = rows // marks
+
+    @pl.when(step == 0)
+    def _():
+        greet()
+
     x = tok_ref[0]
     row = lax.broadcasted_iota(jnp.int32, (marks, rows), 0)
     col = lax.broadcasted_iota(jnp.int32, (marks, rows), 1)
@@ -81,38 +153,143 @@
             low = p.astype(bf16)
             out[0, :, c : c + 256] = low
             if part < 2:
-                (ql_ref, kl_ref)[part][0, :, c : c + 256] = dot(mean, low).astype(bf16)
+                land[step, part, :, c : c + 256] = dot(mean, low).astype(bf16)
+            else:
+                rim[step, 0, :, c : c + 256] = low[rows - RIM :]
+                rim[step, 1, :, c : c + 256] = low[:RIM]
+
+    def copies(s):
+        spot = land_out.at[s, :, pl.ds(me * marks, marks)]
+        sends = [
+            remote(land.at[s], spot, send.at[s, o], recv.at[s, o], {"seq": peer}) for o, peer in seq_peers()
+        ]
+        return sends, pltpu.make_async_copy(land.at[s], spot, local.at[s])
+
+    def rim_copy(s, side):
+        there = lax.rem(me + (1 if side == 0 else count - 1), count)
+        return remote(
+            rim.at[s, side], rim_out.at[s, side], rim_send.at[s, side], rim_recv.at[s, side], {"seq": there}
+        )
+
+    begin(copies(step))
+    for side in range(2):
+        rim_copy(step, side).start()
+
+    @pl.when(step == seqs - 1)
+    def _():
+        def drain(s, carry):
+            finish(copies(s))
+            for side in range(2):
+                rim_copy(s, side).wait()
+            return carry
+
+        lax.fori_loop(0, seqs, drain, 0)
 
 
 def project(tokens, w_qkv, marks):
     seqs, rows, features = tokens.shape
+    ranks = lax.axis_size("seq")
     full = pl.BlockSpec((1, rows, features), lambda s: (s, 0, 0))
-    land = pl.BlockSpec((1, marks, features), lambda s: (s, 0, 0))
+    dma = pltpu.SemaphoreType.DMA
     return pl.pallas_call(
         project_kernel,
         grid=(seqs,),
-        in_specs=[full, pl.BlockSpec(w_qkv.shape, lambda s: (0, 0))],
-        out_specs=[full] * 3 + [land] * 2,
+        in_specs=[full, pl.BlockSpec(w_qkv.shape, lambda s: (0, 0), pipeline_mode=pl.Buffered(1))],
+        out_specs=[full] * 3 + [ANY] * 2,
         out_shape=[jax.ShapeDtypeStruct(tokens.shape, bf16)] * 3
-        + [jax.ShapeDtypeStruct((seqs, marks, features), bf16)] * 2,
-        compiler_params=params(48 * MB),
+        + [
+            jax.ShapeDtypeStruct((seqs, 2, M, features), bf16),
+            jax.ShapeDtypeStruct((seqs, 2, RIM, features), bf16),
+        ],
+        scratch_shapes=[
+            pltpu.VMEM((seqs, 2, marks, features), bf16), pltpu.VMEM((seqs, 2, RIM, features), bf16),
+            dma((seqs, ranks)), dma((seqs, ranks)), dma((seqs,)), dma((seqs, 2)), dma((seqs, 2)), dma((seqs,)),
+        ],
+        compiler_params=params(48 * MB, collective_id=0, has_side_effects=True),
         name="project",
     )(tokens, w_qkv)
 
 
-def scores_kernel(q_ref, k_ref, v_ref, ql_ref, kl_ref, w_ref, p_ref, num_ref, stat_ref):
+def fill_pad(pad, x_ref, rim_ref):
+    rows = x_ref.shape[1]
+    me, count = seq_place()
+    pad[0:RIM, :] = jnp.where(me > 0, rim_ref[0, 0].astype(f32), 0.0)
+    pad[RIM : RIM + rows, :] = x_ref[0].astype(f32)
+    pad[RIM + rows : RIM + rows + RIM, :] = jnp.where(me < count - 1, rim_ref[0, 1].astype(f32), 0.0)
+
+
+def conv_tile(v_ref, rim_ref, f_ref, o_ref, pad):
+    rows = v_ref.shape[1]
+    fill_pad(pad, v_ref, rim_ref)
+    for c in range(0, rows, 64):
+        acc = jnp.zeros((64, 128), f32)
+        for j in range(KW):
+            acc = acc + f_ref[j : j + 1, :] * pad[c + j : c + j + 64, :]
+        o_ref[0, c : c + 64, :] = acc.astype(bf16)
+
+
+def conv_specs(rows, first_step, first_group, groups):
+    at = lambda i: jnp.maximum(i - first_step, 0)
+    seq = lambda i: at(i) // groups
+    group = lambda i: at(i) % groups
+    return (
+        pl.BlockSpec((1, rows, 128), lambda i: (seq(i), 0, first_group + group(i))),
+        pl.BlockSpec((1, 2, RIM, 128), lambda i: (seq(i), 0, 0, first_group + group(i))),
+        pl.BlockSpec((KW, 128), lambda i: (0, first_group + group(i))),
+        pl.BlockSpec((1, rows, 128), lambda i: (seq(i), 0, group(i))),
+    )
+
+
+def conv_back_kernel(g_ref, rim_ref, v_ref, f_ref, o_ref, gf_ref, pad, facc):
+    rows = v_ref.shape[1]
+    fill_pad(pad, g_ref, rim_ref)
+
+    @pl.when(pl.program_id(1) == 0)
+    def _():
+        facc[...] = jnp.zeros_like(facc)
+
+    for c in range(0, rows, 64):
+        acc = jnp.zeros((64, 128), f32)
+        vals = v_ref[0, c : c + 64, :].astype(f32)
+        for j in range(KW):
+            moved = pad[c + 2 * RIM - j : c + 2 * RIM - j + 64, :]
+            acc = acc + f_ref[j : j + 1, :] * moved
+            facc[8 * j : 8 * j + 8, :] += (vals * moved).reshape(8, 8, 128).sum(0)
+        o_ref[0, c : c + 64, :] = acc.astype(bf16)
+
+    @pl.when(pl.program_id(1) == pl.num_programs(1) - 1)
+    def _():
+        gf_ref[...] = facc[...].reshape(KW, 8, 128).sum(1)
+
+
+def conv_back(g, rim, v, taps):
+    seqs, rows, features = v.shape
+    sp = lambda n: pl.BlockSpec((1, n, 128), lambda g, s: (s, 0, g))
+    fs = pl.BlockSpec((KW, 128), lambda g, s: (0, g))
+    return pl.pallas_call(
+        conv_back_kernel,
+        grid=(features // 128, seqs),
+        in_specs=[sp(rows), pl.BlockSpec((1, 2, RIM, 128), lambda g, s: (s, 0, 0, g)), sp(rows), fs],
+        out_specs=[sp(rows), fs],
+        out_shape=[jax.ShapeDtypeStruct(v.shape, bf16), jax.ShapeDtypeStruct((KW, features), f32)],
+        scratch_shapes=[pltpu.VMEM((rows + 2 * RIM, 128), f32), pltpu.VMEM((KW * 8, 128), f32)],
+        name="conv_back",
+    )(g, rim, v, taps)
+
+
+def score_step(step, q_ref, k_ref, v_ref, land_ref, w_ref, p_ref, num_ref, stat_ref):
     rows, features = q_ref.shape[1:]
+    pairs = features // 128
     masks = group_masks((M, 4 * E), 4, bf16)
     masks_wide = group_masks((M, 4 * E), 4, f32)
     ones = jnp.where(
         lane_group((4 * E, 4 * E)) == lax.broadcasted_iota(jnp.int32, (4 * E, 4 * E), 0) // E, 1.0, 0.0
     ).astype(bf16)
-    stat_ref[...] = jnp.zeros_like(stat_ref)
     chunk = min(128, rows)
     upper = lax.broadcasted_iota(jnp.int32, (chunk, 2 * E), 1) >= E
     for g in range(features // 256):
         sl = slice(256 * g, 256 * g + 256)
-        s3 = dot_nt(k_ref[0, :, sl], block_diag(ql_ref[0, :, sl], masks))
+        s3 = dot_nt(k_ref[0, :, sl], block_diag(land_ref[0, 0, :, sl], masks))
         peak = jnp.max(s3, axis=0, keepdims=True)
         e3 = jnp.exp(s3 - peak)
         total = jnp.sum(e3, axis=0, keepdims=True)
@@ -121,10 +298,11 @@
         num = diag_blocks(dot_tn(low, v_ref[0, :, sl]), masks_wide).astype(bf16)
         for i in range(2):
             lanes = slice(128 * i, 128 * i + 128)
-            num_ref[2 * g + i] = num[:, lanes]
-            stat_ref[2 * g + i, 0:1, :] = peak[:, lanes]
-            stat_ref[2 * g + i, 1:2, :] = total[:, lanes]
-        kd = block_diag(kl_ref[0, :, sl], masks)
+            num_ref[step * pairs + 2 * g + i] = num[:, lanes]
+            stat_ref[step * pairs + 2 * g + i] = jnp.concatenate(
+                [peak[:, lanes], total[:, lanes], jnp.zeros((6, 128), f32)], axis=0
+            )
+        kd = block_diag(land_ref[0, 1, :, sl], masks)
         for r in range(0, rows, chunk):
             s1 = dot_nt(q_ref[0, r : r + chunk, sl], kd)
             parts = []
@@ -137,96 +315,66 @@
             p_ref[0, r : r + chunk, sl] = (e1 / dot(e1.astype(bf16), ones)).astype(bf16)
 
 
-def scores(q, k, v, q_land, k_land):
+def scores_kernel(
+    seqs, q_ref, k_ref, v_ref, land_ref, cv_ref, rim_ref, f_ref, w_ref, p_ref, co_ref, num_out, stat_out,
+    num, stat, pad, num_sems, stat_sems,
+):
+    step = pl.program_id(0)
+    steps = pl.num_programs(0)
+    own = num_out.shape[1]
+    pairs = q_ref.shape[2] // 128
+
+    @pl.when(step == 0)
+    def _():
+        greet()
+        if num.shape[0] > seqs * pairs:
+            num[seqs * pairs :] = jnp.zeros_like(num[seqs * pairs :])
+            stat[seqs * pairs :] = jnp.zeros_like(stat[seqs * pairs :])
+
+    @pl.when(step < seqs)
+    def _():
+        score_step(step, q_ref, k_ref, v_ref, land_ref, w_ref, p_ref, num, stat)
+
+    @pl.when(step == seqs - 1)
+    def _():
+        begin(swap_copies(num, num_out, own, num_sems))
+        begin(swap_copies(stat, stat_out, own, stat_sems))
+
+    @pl.when(step >= seqs)
+    def _():
+        conv_tile(cv_ref, rim_ref, f_ref, co_ref, pad)
+
+    @pl.when(step == steps - 1)
+    def _():
+        finish(swap_copies(num, num_out, own, num_sems))
+        finish(swap_copies(stat, stat_out, own, stat_sems))
+
+
+def scores(q, k, v, land, rim, taps, own, groups):
     seqs, rows, features = q.shape
-    pairs = features // 128
-    full = pl.BlockSpec((1, rows, features), lambda s: (s, 0, 0))
-    land = pl.BlockSpec((1, M, features), lambda s: (s, 0, 0))
+    ranks = lax.axis_size("seq")
+    here = lambda i: jnp.minimum(i, seqs - 1)
+    full = pl.BlockSpec((1, rows, features), lambda i: (here(i), 0, 0))
+    cv, rims, ft, co = conv_specs(rows, seqs, 0, groups)
     return pl.pallas_call(
-        scores_kernel,
-        grid=(seqs,),
-        in_specs=[full] * 3 + [land] * 2,
-        out_specs=[full] * 2
-        + [
-            pl.BlockSpec((pairs, M, 128), lambda s: (s, 0, 0)),
-            pl.BlockSpec((pairs, 8, 128), lambda s: (s, 0, 0)),
-        ],
+        functools.partial(scores_kernel, seqs),
+        grid=(seqs + seqs * groups,),
+        in_specs=[full] * 3
+        + [pl.BlockSpec((1, 2, M, features), lambda i: (here(i), 0, 0, 0)), cv, rims, ft],
+        out_specs=[full] * 2 + [co, ANY, ANY],
         out_shape=[jax.ShapeDtypeStruct(q.shape, bf16)] * 2
         + [
-            jax.ShapeDtypeStruct((seqs * pairs, M, 128), bf16),
-            jax.ShapeDtypeStruct((seqs * pairs, 8, 128), f32),
-        ],
-        compiler_params=params(48 * MB),
+            jax.ShapeDtypeStruct((seqs, rows, 128 * groups), bf16),
+            jax.ShapeDtypeStruct((ranks, own, M, 128), bf16),
+            jax.ShapeDtypeStruct((ranks, own, 8, 128), f32),
+        ],
+        scratch_shapes=[
+            pltpu.VMEM((ranks * own, M, 128), bf16), pltpu.VMEM((ranks * own, 8, 128), f32),
+            pltpu.VMEM((rows + 2 * RIM, 128), f32), rank_sems(), rank_sems(),
+        ],
+        compiler_params=params(48 * MB, collective_id=1, has_side_effects=True),
         name="scores",
-    )(q, k, v, q_land, k_land)
-
-
-def fill_pad(pad, x_ref, l_ref, r_ref):
-    rows = x_ref.shape[1]
-    pad[0:RIM, :] = l_ref[0].astype(f32)
-    pad[RIM : RIM + rows, :] = x_ref[0].astype(f32)
-    pad[RIM + rows : RIM + rows + RIM, :] = r_ref[0].astype(f32)
-
-
-def conv_kernel(v_ref, l_ref, r_ref, f_ref, o_ref, pad):
-    rows = v_ref.shape[1]
-    fill_pad(pad, v_ref, l_ref, r_ref)
-    for c in range(0, rows, 64):
-        acc = jnp.zeros((64, 128), f32)
-        for j in range(KW):
-            acc = acc + f_ref[j : j + 1, :] * pad[c + j : c + j + 64, :]
-        o_ref[0, c : c + 64, :] = acc.astype(bf16)
-
-
-def conv(v, left, right, taps):
-    seqs, rows, features = v.shape
-    sp = lambda n: pl.BlockSpec((1, n, 128), lambda s, g: (s, 0, g))
-    return pl.pallas_call(
-        conv_kernel,
-        grid=(seqs, features // 128),
-        in_specs=[sp(rows), sp(RIM), sp(RIM), pl.BlockSpec((KW, 128), lambda s, g: (0, g))],
-        out_specs=sp(rows),
-        out_shape=jax.ShapeDtypeStruct(v.shape, bf16),
-        scratch_shapes=[pltpu.VMEM((rows + 2 * RIM, 128), f32)],
-        name="conv",
-    )(v, left, right, taps)
-
-
-def conv_back_kernel(g_ref, l_ref, r_ref, v_ref, f_ref, o_ref, gf_ref, pad, facc):
-    rows = v_ref.shape[1]
-    fill_pad(pad, g_ref, l_ref, r_ref)
-
-    @pl.when(pl.program_id(1) == 0)
-    def _():
-        facc[...] = jnp.zeros_like(facc)
-
-    for c in range(0, rows, 64):
-        acc = jnp.zeros((64, 128), f32)
-        vals = v_ref[0, c : c + 64, :].astype(f32)
-        for j in range(KW):
-            moved = pad[c + 2 * RIM - j : c + 2 * RIM - j + 64, :]
-            acc = acc + f_ref[j : j + 1, :] * moved
-            facc[8 * j : 8 * j + 8, :] += (vals * moved).reshape(8, 8, 128).sum(0)
-        o_ref[0, c : c + 64, :] = acc.astype(bf16)
-
-    @pl.when(pl.program_id(1) == pl.num_programs(1) - 1)
-    def _():
-        gf_ref[...] = facc[...].reshape(KW, 8, 128).sum(1)
-
-
-def conv_back(g, left, right, v, taps):
-    seqs, rows, features = v.shape
-    sp = lambda n: pl.BlockSpec((1, n, 128), lambda g, s: (s, 0, g))
-    fs = pl.BlockSpec((KW, 128), lambda g, s: (0, g))
-    return pl.pallas_call(
-        conv_back_kernel,
-        grid=(features // 128, seqs),
-        in_specs=[sp(rows), sp(RIM), sp(RIM), sp(rows), fs],
-        out_specs=[sp(rows), fs],
-        out_shape=[jax.ShapeDtypeStruct(v.shape, bf16), jax.ShapeDtypeStruct((KW, features), f32)],
-        scratch_shapes=[pltpu.VMEM((rows + 2 * RIM, 128), f32), pltpu.VMEM((KW * 8, 128), f32)],
-        name="conv_back",
-    )(g, left, right, v, taps)
+    )(q, k, v, land, v, rim, taps)
 
 
 def split(x):
@@ -288,8 +436,15 @@
     return lane >= E, row == lane % E, group_masks((M, 128), 2, bf16), group_masks((M, 128), 2, f32)
 
 
-def inverse_kernel(
-    num_ref, stat_ref, ql_ref, kl_ref, mixed_ref, sum_ref, mid_ref, z_ref, p_ref, a_ref, w_ref,
+def own_pair(land_ref, i, own):
+    me, _ = seq_place()
+    per = land_ref.shape[2] // 128
+    p = jnp.minimum(me * own + i, land_ref.shape[0] * per - 1)
+    return land_ref[p // per, :, pl.ds(pl.multiple_of((p % per) * 128, 128), 128)]
+
+
+def inverse_step(
+    num_ref, stat_ref, land_ref, mixed_ref, sum_ref, mid_ref, z_ref, p_ref, a_ref, w_ref,
     scale_ref, tot_ref, alpha_ref,
 ):
     ranks, own = num_ref.shape[:2]
@@ -309,7 +464,7 @@
         total = to_column(total, same, upper)
         tot_ref[i] = total
         sum_ref[i] = numer / total
-        ql, kl = ql_ref[i], kl_ref[i]
+        ql, kl = own_pair(land_ref.at[:, 0], i, own), own_pair(land_ref.at[:, 1], i, own)
         s2 = dot_nt(ql, block_diag(kl, masks))
         e2 = jnp.exp(s2 - half_reduce(s2, upper, jnp.max, -jnp.inf))
         middle = e2 / half_reduce(e2, upper, jnp.sum, 0.0)
@@ -340,23 +495,63 @@
         mixed_ref[i] = pair_nn([z_ref[NEWTON, i]], sum_ref[i], masks)[0].astype(bf16)
 
 
-def inverse(num, stat, ql, kl):
+def inverse_kernel(
+    num_ref, stat_ref, land_ref, cv_ref, rim_ref, f_ref, mixed_out, co_ref, sum_ref, mid_ref, z_ref, p_ref,
+    a_ref, w_ref, scale_ref, tot_ref, alpha_ref, mixed, pad, sems,
+):
+    step = pl.program_id(0)
+    own = num_ref.shape[1]
+
+    @pl.when(step == 0)
+    def _():
+        greet()
+        inverse_step(
+            num_ref, stat_ref, land_ref, mixed, sum_ref, mid_ref, z_ref, p_ref, a_ref, w_ref, scale_ref,
+            tot_ref, alpha_ref,
+        )
+        begin(spread_copies(mixed, mixed_out, own, sems))
+
+    @pl.when(step > 0)
+    def _():
+        conv_tile(cv_ref, rim_ref, f_ref, co_ref, pad)
+
+    @pl.when(step == pl.num_programs(0) - 1)
+    def _():
+        finish(spread_copies(mixed, mixed_out, own, sems))
+
+
+def inverse(num, stat, land, v, rim, taps, first_group):
     ranks, own = num.shape[:2]
+    seqs, rows, features = v.shape
+    groups = features // 128 - first_group
     mat = jax.ShapeDtypeStruct((own, M, 128), f32)
     steps = lambda n: jax.ShapeDtypeStruct((n, own, M, 128), f32)
+    whole = lambda a: pl.BlockSpec(a.shape, lambda i: (0,) * len(a.shape), pipeline_mode=pl.Buffered(1))
+    saved = [
+        mat, mat, steps(NEWTON + 1), steps(NEWTON), steps(NEWTON), steps(NEWTON),
+        jax.ShapeDtypeStruct((own, 8, 128), f32), mat, steps(ranks),
+    ]
+    cv, rims, ft, co = conv_specs(rows, 1, first_group, groups)
     return pl.pallas_call(
         inverse_kernel,
+        grid=(1 + seqs * groups,),
+        in_specs=[whole(num), whole(stat), whole(land), cv, rims, ft],
+        out_specs=[ANY, co] + [whole(a) for a in saved],
         out_shape=[
-            jax.ShapeDtypeStruct((own, M, 128), bf16), mat, mat, steps(NEWTON + 1), steps(NEWTON),
-            steps(NEWTON), steps(NEWTON), jax.ShapeDtypeStruct((own, 8, 128), f32), mat, steps(ranks),
-        ],
-        compiler_params=params(48 * MB),
+            jax.ShapeDtypeStruct((ranks * own, M, 128), bf16),
+            jax.ShapeDtypeStruct((seqs, rows, 128 * groups), bf16),
+        ]
+        + saved,
+        scratch_shapes=[
+            pltpu.VMEM((own, M, 128), bf16), pltpu.VMEM((rows + 2 * RIM, 128), f32), rank_sems(),
+        ],
+        compiler_params=params(48 * MB, collective_id=2, has_side_effects=True),
         name="inverse",
-    )(num, stat, ql, kl)
+    )(num, stat, land, v, rim, taps)
 
 
 def inverse_back_kernel(
-    land_ref, ql_ref, kl_ref, sum_ref, mid_ref, z_ref, p_ref, a_ref, w_ref, scale_ref, tot_ref,
+    land_ref, marks_ref, sum_ref, mid_ref, z_ref, p_ref, a_ref, w_ref, scale_ref, tot_ref,
     alpha_ref, gn_ref, gt_ref, mq_ref, mk_ref, g_ref, dk_ref,
 ):
     ranks, own = land_ref.shape[:2]
@@ -407,13 +602,13 @@
         dk = dk_ref[i] + turned * scale - share * (d_scale * scale * scale)
         ds = middle * (dk - half_reduce(middle * dk, upper, jnp.sum, 0.0))
         hi, lo = split(ds)
-        both = dot(jnp.concatenate([hi, lo], axis=0), block_diag(kl_ref[i], masks))
+        both = dot(jnp.concatenate([hi, lo], axis=0), block_diag(own_pair(marks_ref.at[:, 1], i, own), masks))
         mq_ref[i] = both[:M] + both[M:]
-        turned = dot_tn(jnp.concatenate([hi, lo], axis=1), ql_ref[i])
+        turned = dot_tn(jnp.concatenate([hi, lo], axis=1), own_pair(marks_ref.at[:, 0], i, own))
         mk_ref[i] = diag_blocks(turned[:128] + turned[128:], masks_wide)
 
 
-def inverse_back(land, ql, kl, saved):
+def inverse_back(land, marks, saved):
     ranks, own = land.shape[:2]
     mat = jax.ShapeDtypeStruct((own, M, 128), f32)
     return pl.pallas_call(
@@ -425,7 +620,7 @@
         scratch_shapes=[pltpu.VMEM((own, M, 128), f32)] * 2,
         compiler_params=params(48 * MB),
         name="inverse_back",
-    )(land, ql, kl, *saved)
+    )(land, marks, *saved)
 
 
 def mean_of(x):
@@ -445,7 +640,7 @@
 
 
 def row_kernel(
-    tok_ref, p_ref, conv_ref, mix_ref, top_ref, w_out_ref, w_up_ref, w_down_ref, ga_ref, gf_ref,
+    tok_ref, p_ref, conv_a_ref, conv_b_ref, mix_ref, top_ref, w_out_ref, w_up_ref, w_down_ref, ga_ref, gf_ref,
     out_ref, proj_ref, gm_ref, wg_ref, gains_ref,
     act, gul, slope, hid_t, gdl_t, mix_t, gpr, resid,
 ):
@@ -467,9 +662,11 @@
         for g in range(features // 256):
             sl = slice(256 * g, 256 * g + 256)
             att = dot(p_ref[:, sl], block_diag(mix_ref[0, :, sl], masks))
-            low = (att + conv_ref[:, sl].astype(f32)).astype(bf16)
-            resid[:, sl] = low
-        mixed = resid[...]
+            resid[:, sl] = att
+        half = conv_a_ref.shape[1]
+        resid[:, :half] += conv_a_ref[...].astype(f32)
+        resid[:, half:] += conv_b_ref[...].astype(f32)
+        mixed = resid[...].astype(bf16)
         mix_t[:, rows] = mixed.T
         residual = tok_ref[...].astype(f32) + dot(mixed, w_out_ref[...])
         centre = residual - mean_of(residual)
@@ -525,7 +722,7 @@
                 wg_ref[0, :, c : c + 256] = dot(left[...], right[:, cols]).astype(bf16)
 
 
-def row_pass(tokens, probs, conv_out, mixed, grad_out, w_out, w_up, w_down, gain_att, gain_ffn):
+def row_pass(tokens, probs, conv_a, conv_b, mixed, grad_out, w_out, w_up, w_down, gain_att, gain_ffn):
     seqs, rows, features = tokens.shape
     ff = w_up.shape[1]
     size = min(256, rows)
@@ -535,7 +732,8 @@
     here = lambda i: jnp.minimum(i, blocks - 1)
     block = pl.BlockSpec((size, features), lambda i: (here(i), 0))
     whole = lambda a: pl.BlockSpec(a.shape, lambda i: (0,) * a.ndim, pipeline_mode=pl.Buffered(1))
-    flat = lambda a: a.reshape(total, features)
+    flat = lambda a: a.reshape(total, a.shape[2])
+    part = lambda a: pl.BlockSpec((size, a.shape[2]), lambda i: (here(i), 0))
     gains = [gain_att.reshape(1, features), gain_ffn.reshape(1, features)]
     row_out = jax.ShapeDtypeStruct((total, features), bf16)
     tall = pltpu.VMEM((features, total), bf16)
@@ -543,7 +741,7 @@
         row_kernel,
         grid=(blocks + grads,),
         in_specs=[
-            block, block, block,
+            block, block, part(conv_a), part(conv_b),
             pl.BlockSpec((1, M, features), lambda i: (here(i) * size // rows, 0, 0)),
             block, whole(w_out), whole(w_up), whole(w_down), whole(gains[0]), whole(gains[1]),
         ],
@@ -559,11 +757,11 @@
         ],
         scratch_shapes=[
             pltpu.VMEM((total, ff), bf16), pltpu.VMEM((total, ff), bf16), pltpu.VMEM((size, ff), bf16),
-            tall, tall, tall, pltpu.VMEM((total, features), bf16), pltpu.VMEM((size, features), bf16),
+            tall, tall, tall, pltpu.VMEM((total, features), bf16), pltpu.VMEM((size, features), f32),
         ],
         compiler_params=params(60 * MB),
         name="row_pass",
-    )(flat(tokens), flat(probs), flat(conv_out), mixed, flat(grad_out), w_out, w_up, w_down, *gains)
+    )(flat(tokens), flat(probs), flat(conv_a), flat(conv_b), mixed, flat(grad_out), w_out, w_up, w_down, *gains)
 
 
 def first_back_kernel(gm_ref, p_ref, q_ref, mix_ref, kl_ref, land_ref, gq_ref, klp_ref):
@@ -707,7 +905,7 @@
     head, tail = cells[:, :width], cells[:, cells.shape[1] - width :]
     left = lax.ppermute(tail, "seq", [(i, i + 1) for i in range(count - 1)])
     right = lax.ppermute(head, "seq", [(i + 1, i) for i in range(count - 1)])
-    return left, right
+    return jnp.stack([left, right], axis=1)
 
 
 def scatter_sum(grad):
@@ -724,10 +922,6 @@
     pairs = seqs * (features // 128)
     own = -(-pairs // ranks)
 
-    def to_pairs(x):
-        x = x.reshape(seqs, M, features // 128, 128).transpose(0, 2, 1, 3)
-        return x.reshape(pairs, M, 128)
-
     def from_pairs(x):
         x = x[:pairs].reshape(seqs, features // 128, M, 128).transpose(0, 2, 1, 3)
         return x.reshape(seqs, M, features)
@@ -739,22 +933,15 @@
         out = lax.all_to_all(pad_pairs(x), "seq", 0, 0, tiled=True)
         return out.reshape((ranks, own) + x.shape[1:])
 
-    def mine(x):
-        return lax.dynamic_slice_in_dim(pad_pairs(x), rank * own, own, 0)
-
-    q, k, v, q_part, k_part = project(tokens, w_qkv, marks)
-    land = lax.all_gather(jnp.stack([q_part, k_part]), "seq", axis=2, tiled=True)
-    q_land, k_land = land[0], land[1]
-    v_left, v_right = halo(v, RIM)
     taps = conv_filter.astype(f32)
-    weights, probs, num, stat = scores(q, k, v, q_land, k_land)
-    num_parts, stat_parts = exchange(num), exchange(stat)
-    conv_out = conv(v, v_left, v_right, taps)
-    ql_own, kl_own = mine(to_pairs(q_land)), mine(to_pairs(k_land))
-    mixed_own, *saved = inverse(num_parts, stat_parts, ql_own, kl_own)
-    mixed = from_pairs(lax.all_gather(mixed_own, "seq", axis=0, tiled=True))
+    q, k, v, land, v_rim = project(tokens, w_qkv, marks)
+    q_land, k_land = land[:, 0], land[:, 1]
+    first_group = features // 256
+    weights, probs, conv_a, num_parts, stat_parts = scores(q, k, v, land, v_rim, taps, own, first_group)
+    mixed_pairs, conv_b, *saved = inverse(num_parts, stat_parts, land, v, v_rim, taps, first_group)
+    mixed = from_pairs(mixed_pairs)
     layer_out, proj, gm, wg, gains = row_pass(
-        tokens, probs, conv_out, mixed, grad_out, w_out, w_up, w_down, gain_att, gain_ffn
+        tokens, probs, conv_a, conv_b, mixed, grad_out, w_out, w_up, w_down, gain_att, gain_ffn
     )
     shape3 = (seqs, rows, features)
     gm = gm.reshape(shape3)
@@ -763,10 +950,10 @@
     down_share = scatter_sum(wg[chunks : 2 * chunks].transpose(0, 2, 1).reshape(ff, features))
     out_share = scatter_sum(wg[2 * chunks])
     land_part, gq, k_land_part = first_back(gm, probs, q, mixed, k_land)
-    g_left, g_right = halo(gm, RIM)
+    g_rim = halo(gm, RIM)
     land_parts = exchange(land_part)
-    grad_conv, taps_grad = conv_back(gm, g_left, g_right, v, taps)
-    gn_own, gt_own, mid_q, mid_k = inverse_back(land_parts, ql_own, kl_own, saved)
+    grad_conv, taps_grad = conv_back(gm, g_rim, v, taps)
+    gn_own, gt_own, mid_q, mid_k = inverse_back(land_parts, land, saved)
 
     def give_back(x):
         x = x.reshape((ranks * own,) + x.shape[2:])

time: 627 us -> 597 us (0.952)
  blocking collectives: 46.9 us -> 14.6 us
  Pallas kernels: 210 us -> 233 us
  starting transfers between devices: 33.9 us -> 18.9 us
  waiting for transfers between devices: 224 us -> 216 us
    all_gather x2 -> x0, blocking collectives: 32.2 us -> none  [the longest x1 18.2 us: per_device(): lax.all_gather(jnp.stack([q_part, k_part]), 'seq', axis=2, tiled=True)]
    pallas_call x1, Pallas kernels: 15.6 us -> 28 us  [project(): pl.pallas_call(project_kernel, grid=(seqs,), in_specs=[full, pl.BlockSpec...]
    pallas_call x3 -> x2, Pallas kernels: 35.8 us -> 46.2 us  [the longest x1 29 us: scores(): pl.pallas_call(functools.partial(scores_kernel, seqs), grid=(seqs + seqs...]
    all_to_all x3 -> x1, starting transfers between devices: 12.7 us -> 3.45 us  [exchange(): out = lax.all_to_all(pad_pairs(x), 'seq', 0, 0, tiled=True)]
    unnamed x72 -> x68, local copies, waits for them, and re-layouts: 44 us -> 46.7 us
  transfers between devices with their start and end apart: 18 -> 14, of which waited for: 12 -> 10; matrix products, arithmetic and copies ran while one was open for 10% -> 11% of each run, Pallas kernels for 14% -> 12%
where the time goes in v2:
time: 597 us; the launch traced here: 588 us
  Pallas kernels  233 us (39%)
  waiting for transfers between devices  216 us (36%)
  local copies, waits for them, and re-layouts  85.8 us (14%)
  starting transfers between devices  18.9 us (3%)
  between operations  16.4 us (3%)
  blocking collectives  14.6 us (2%)
    unnamed x13, waiting for transfers between devices  107 us
    pallas_call x1, Pallas kernels, row_pass(): pl.pallas_call(row_kernel, grid=(blocks + grads,), in_specs=[block, block...  84.1 us
    reduce_scatter x2, waiting for transfers between devices, scatter_sum(): share = lax.psum_scatter(grad, 'dp', scatter_dimension=0, tiled=True)  55.6 us
    unnamed x68, local copies, waits for them, and re-layouts  46.7 us
    reduce_scatter x2, waiting for transfers between devices, scatter_sum(): lax.psum_scatter(share, 'seq', scatter_dimension=1, tiled=True).astype(f32)  42.9 us
    pallas_call x1, Pallas kernels, scores(): pl.pallas_call(functools.partial(scores_kernel, seqs), grid=(seqs + seqs...  29 us
    pallas_call x1, Pallas kernels, project(): pl.pallas_call(project_kernel, grid=(seqs,), in_specs=[full, pl.BlockSpec...  28 us
    pallas_call x1, Pallas kernels, last_pass(): pl.pallas_call(last_kernel, grid=(seqs + 3,), in_specs=[full] * 4 + [land...  26.4 us
  transfers between devices with their start and end apart: 14, of which 10 were waited for; matrix products, arithmetic and copies ran while one was open for 11% of the time, Pallas kernels for 12%

profile of v2, /device:TPU:0, one launch (start us, length us, event | category | flops | bytes accessed | tf_op | source)
XLA Modules:
  0.0 588.0 jit_solution(121754296781188464)
XLA Ops:
  8.9 28.0 %project.1 = (bf16[3,512,768]{2,1,0:T(8,128)(2,1)S(1)}, bf16[3,512,768]{2,1,0:T(8,128)(2,1)S(1)}, bf16[3,512,768]{2,1,0:T(8,128)(2,1)}, bf16[3,2,64,768]{3,2,1,0:T(8,128)(2,1)S(1)}, bf16[3,2,16,768]{3,2,1,0:T(8,128)(2,1)S(1)}) custom-call(bf16[3,512,768]{2,1,0:T(8,128)(2,1)} %tok_ref.3, bf16[768,2304]{1,0:T(8,128)(2,1)} %w_ref.3), custom_call_target="tpu_custom_call" | custom-call | tf_op jit(solution)/shard_map/project/pallas_call | solution.py:194
  36.9 1.4 copy-done.1
  38.3 1.4 copy-done.2
  39.7 29.0 %scores.1 = (bf16[3,512,768]{2,1,0:T(8,128)(2,1)S(1)}, bf16[3,512,768]{2,1,0:T(8,128)(2,1)}, bf16[3,512,384]{2,1,0:T(8,128)(2,1)S(1)}, bf16[4,5,64,128]{3,2,1,0:T(8,128)(2,1)S(1)}, f32[4,5,8,128]{3,2,1,0:T(8,128)S(1)}) custom-call(bf16[3,512,768]{2,1,0:T(8,128)(2,1)} %copy-done.2, bf16[3,512,768]{2,1,0:T(8,128)(2,1)} %copy-done.1, ...), custom_call_target="tpu_custom_call" | custom-call | tf_op jit(solution)/shard_map/scores/pallas_call | solution.py:359
  68.8 1.4 copy-done.4
  71.3 17.1 %inverse.1 = (bf16[20,64,128]{2,1,0:T(8,128)(2,1)S(1)}, bf16[3,512,384]{2,1,0:T(8,128)(2,1)}, f32[5,64,128]{2,1,0:T(8,128)S(1)}, f32[5,64,128]{2,1,0:T(8,128)S(1...) custom-call(bf16[4,5,64,128]{3,2,1,0:T(8,128)(2,1)S(1)} %get-tuple-e, ...), custom_call_target="tpu_custom_call" | custom-call | tf_op jit(solution)/shard_map/inverse/pallas_call | solution.py:535
  92.0 2.1 reshape.99.mix_ref
  95.2 84.1 %row_pass.1 = (bf16[1536,768]{1,0:T(8,128)(2,1)}, bf16[1536,768]{1,0:T(8,128)(2,1)}, bf16[1536,768]{1,0:T(8,128)(2,1)}, bf16[9,768,768]{2,1,0:T(8,128)(2,1)}, f32[16,768]{1,0:T(8,128)}) custom-call(bf16[1536,768]{1,0:T(8,128)(2,1)} %bitcast.71, bf16[1536,768]{1,0:T(8,128)(2,1)} %bitcast.75, bf16[1536,384]{1,0:T(8,128)(2,1)} %bitcast.70, ...), custom_call_target="tpu_custom_call" | custom-call | tf_op jit(solution)/shard_map/row_pass/pallas_call | solution.py:740
  179.3 1.7 copy-done
  181.0 6.6 %first_back.1 = (bf16[18,64,128]{2,1,0:T(8,128)(2,1)S(1)}, bf16[3,512,768]{2,1,0:T(8,128)(2,1)S(1)}, f32[3,64,768]{2,1,0:T(8,128)S(1)}) custom-call(bf16[3,512,768]{2,1,0:T(8,128)(2,1)S(1)} %bitcast.68, bf16[3,512,768]{2,1,0:T(8,128)(2,1)} %get-tuple-element.54.p_ref, bf16[3,512,768]{2,1,0:T(8,128)(2,1)} %copy-done.2, bf16[3,64,768]{2,1,0:T(8,128)(2,1)S(1)} %copy-done.3, ...), custom_call_target="tpu_custom_call" | custom-call | tf_op jit(solution)/shard_map/first_back/pallas_call | solution.py:792
  187.6 1.4 copy-done.5
  190.5 3.5 all-to-all-start
  194.0 1.6 fusion.2
  195.6 1.3 collective-permute-start.1
  196.9 5.2 collective-permute-start
  202.2 1.2 copy-done.11
  207.2 11.7 %inverse_back.1 = (bf16[4,5,64,128]{3,2,1,0:T(8,128)(2,1)}, f32[4,5,8,128]{3,2,1,0:T(8,128)}, f32[5,64,128]{2,1,0:T(8,128)S(1)}, f32[5,64,128]{2,1,0:T(8,128)S(1)}) custom-call(bf16[4,5,64,128]{3,2,1,0:T(8,128)(2,1)S(1)} %bitcast.69, bf16[3,2,64,768]{3,2,1,0:T(8,128)(2,1)S(1)} %get-tuple-element.52.land_ref.marks_ref, f32[5,64,128]{2,1,0:T(8,128)S(1)} %copy-done.19, ...), custom_call_target="tpu_custom_call" | custom-call | tf_op jit(solution)/shard_map/inverse_back/pallas_call | solution.py:614
  219.6 3.4 all-to-all-start.2
  223.0 2.4 slice_bitcast_fusion.2
  225.5 1.6 pad_maximum_fusion.1.rim_ref
  227.1 23.6 %conv_back.1 = (bf16[3,512,768]{2,1,0:T(8,128)(2,1)}, f32[33,768]{1,0:T(8,128)}) custom-call(bf16[3,512,768]{2,1,0:T(8,128)(2,1)} %bitcast.67, bf16[3,2,16,768]{3,2,1,0:T(8,128)(2,1)} %pad_maximum_fusion.1.rim_ref, bf16[3,512,768]{2,1,0:T(8,128)(2,1)} %get-tuple-element.51.v_ref.cv_ref, f32[33,768]{1,0:T(8,128)} %copy-done.8), custom_call_target="tpu_custom_call" | custom-call | tf_op jit(solution)/shard_map/conv_back/pallas_call | solution.py:269
  250.7 5.2 all-to-all-start.1
  256.4 6.9 %all-to-all-done.1 = bf16[20,64,128]{2,1,0:T(8,128)(2,1)S(1)} async-done(((bf16[20,64,128]{2,1,0:T(8,128)(2,1)}), bf16[20,64,128]{2,1,0:T(8,128)(2,1)S(1)}, u32[]{:S(2)}, u32[]{:S(2)}) %all-to-all-start.1) | async-done | bytes 327712 | tf_op jit(solution)/shard_map/all_to_all | solution.py:960
  263.3 6.0 %third_back.1 = (bf16[3,512,768]{2,1,0:T(8,128)(2,1)S(1)}, bf16[3,512,768]{2,1,0:T(8,128)(2,1)S(1)}, f32[3,64,768]{2,1,0:T(8,128)S(1)}) custom-call(bf16[3,512,768]{2,1,0:T(8,128)(2,1)} %copy-done.4, bf16[3,512,768]{2,1,0:T(8,128)(2,1)} %get-tuple-element.51.v_ref.cv_ref, bf16[3,512,768]{2,1,0:T(8,128)(2,1)} %copy-done.1, ...), custom_call_target="tpu_custom_call" | custom-call | tf_op jit(solution)/shard_map/third_back/pallas_call | solution.py:828
  269.4 14.6 %all_to_all.20 = bf16[4,2,3,16,768]{4,3,2,1,0:T(8,128)(2,1)S(1)} all-to-all(bf16[4,2,3,16,768]{4,3,2,1,0:T(8,128)(2,1)S(1)} %copy_bitcast_fusion), channel_id=1, replica_groups=mesh['dp'=8,'seq'=4] {'seq'}, dimensions={0} | all-to-all | bytes 1179648 | tf_op jit(solution)/shard_map/all_to_all | solution.py:972
  284.9 26.4 %last_pass.1 = (bf16[3,512,768]{2,1,0:T(8,128)(2,1)}, bf16[3,768,768]{2,1,0:T(8,128)(2,1)}) custom-call(bf16[3,512,768]{2,1,0:T(8,128)(2,1)} %tok_ref.3, bf16[3,512,768]{2,1,0:T(8,128)(2,1)} %copy-done.5, bf16[3,512,768]{2,1,0:T(8,128)(2,1)} %copy-done.7, bf16[3,512,768]{2,1,0:T(8,128)(2,1)} %copy-done.6, f32[3,16,768]{2,1,0:T(8,128)} %get-tuple-element.116.qo_ref, ...), custom_call_target="tpu_custom_call" | custom-call | tf_op jit(solution)/shard_map/last_pass/pallas_call | solution.py:885
  311.3 6.1 %copy.42 = bf16[768,3,768]{0,2,1:T(8,128)(2,1)} copy(bf16[768,3,768]{2,0,1:T(8,128)(2,1)} %bitcast.76) | data formatting | bytes 7077888 | tf_op jit(solution)/shard_map/transpose | solution.py:974
  317.3 5.8 copy.48
  323.2 8.1 %slice_bitcast_fusion = (bf16[4,768,768]{1,2,0:T(8,128)(2,1)}, bf16[768,4,768]{2,0,1:T(8,128)(2,1)}) fusion(bf16[9,768,768]{2,1,0:T(8,128)(2,1)} %get-tuple-element.86), kind=kLoop, calls=%fused_computation | loop fusion | bytes 18874368 | tf_op jit(solution)/shard_map/transpose | solution.py:950
  331.3 6.8 %copy.44 = bf16[4,768,768]{2,1,0:T(8,128)(2,1)} copy(bf16[4,768,768]{1,2,0:T(8,128)(2,1)} %get-tuple-element.109) | data formatting | bytes 9437184 | tf_op jit(solution)/shard_map/transpose | solution.py:950
  338.2 6.7 %copy.43 = bf16[768,4,768]{0,2,1:T(8,128)(2,1)} copy(bf16[768,4,768]{2,0,1:T(8,128)(2,1)} %get-tuple-element.110) | data formatting | bytes 9437184 | tf_op jit(solution)/shard_map/transpose | solution.py:949
  344.9 6.6 %copy.52 = bf16[768,3072]{1,0:T(8,128)(2,1)} copy(bf16[768,3072]{0,1:T(8,128)(2,1)} %bitcast.73) | data formatting | bytes 9437184
  353.2 1.7 copy.50
  355.0 15.5 %reduce-scatter.25.cloned.1.call-done = bf16[96,2304]{1,0:T(8,128)(2,1)} async-done(((bf16[768,2304]{1,0:T(8,128)(2,1)}), bf16[96,2304]{1,0:T(8,128)(2,1)}) %reduce-scatter.25.cloned.1.call-update) | async-done | bytes 442384
  370.5 2.1 copy.49
  372.7 55.6 %reduce-scatter.23.cloned.1.call-done = bf16[384,768]{1,0:T(8,128)(2,1)} async-done(((bf16[3072,768]{1,0:T(8,128)(2,1)}), bf16[384,768]{1,0:T(8,128)(2,1)}) %reduce-scatter.23.cloned.1.call-update) | async-done | bytes 589840 | tf_op jit(solution)/shard_map/reduce_scatter | solution.py:912
  428.3 2.1 copy.54
  430.5 55.1 %reduce-scatter.29.cloned.1.call-done = bf16[96,3072]{1,0:T(8,128)(2,1)} async-done(((bf16[768,3072]{1,0:T(8,128)(2,1)}), bf16[96,3072]{1,0:T(8,128)(2,1)}) %reduce-scatter.29.cloned.1.call-update) | async-done | bytes 589840
  485.6 2.2 copy.53
  487.8 3.4 all-reduce.3.cloned.1.call-done
  491.2 1.4 slice_reduce_fusion
  492.7 15.1 %reduce-scatter.27.cloned.1.call-done = bf16[192,96]{1,0:T(8,128)(2,1)} async-done(((bf16[768,96]{1,0:T(8,128)(2,1)}), bf16[192,96]{1,0:T(8,128)(2,1)}) %reduce-scatter.27.cloned.1.call-update) | async-done | bytes 36880
  509.3 20.8 %reduce-scatter.17.cloned.1.call-done = bf16[96,576]{0,1:T(8,128)(2,1)} async-done(((bf16[96,2304]{0,1:T(8,128)(2,1)}), bf16[96,576]{0,1:T(8,128)(2,1)}) %reduce-scatter.17.cloned.1.call-update) | async-done | bytes 110608 | tf_op jit(solution)/shard_map/reduce_scatter | solution.py:913
  530.1 1.7 copy.45
  531.8 21.0 %reduce-scatter.31.cloned.1.call-done = bf16[192,384]{1,0:T(8,128)(2,1)} async-done(((bf16[768,384]{1,0:T(8,128)(2,1)}), bf16[192,384]{1,0:T(8,128)(2,1)}) %reduce-scatter.31.cloned.1.call-update) | async-done | bytes 147472
  554.7 22.1 %reduce-scatter.21.cloned.1.call-done = bf16[96,768]{0,1:T(8,128)(2,1)} async-done(((bf16[96,3072]{0,1:T(8,128)(2,1)}), bf16[96,768]{0,1:T(8,128)(2,1)}) %reduce-scatter.21.cloned.1.call-update) | async-done | bytes 147472 | tf_op jit(solution)/shard_map/reduce_scatter | solution.py:913
  576.8 1.8 copy.46
  578.6 1.6 copy.69
  (99 shorter events, 19.5 us)
Async XLA Ops:
  8.9 62.4 %copy-start.8 = (f32[33,768]{1,0:T(8,128)}, f32[33,768]{1,0:T(8,128)S(1)}, u32[]{:S(2)}) copy-start(f32[33,768]{1,0:T(8,128)S(1)} %convert_element_type.22.f_ref) | copy-start | bytes 304132
  36.9 1.4 copy-start.1
  38.3 1.4 copy-start.2
  68.8 1.4 copy-start.4
  70.2 1.1 copy-start.9
  71.3 22.7 %copy-start.26 = (f32[768]{0:T(1024)S(1)}, f32[768]{0:T(1024)}, u32[]{:S(2)}) copy-start(f32[768]{0:T(1024)} %param.15) | copy-start | bytes 9220
  71.3 23.3 %copy-start.27 = (f32[768]{0:T(1024)S(1)}, f32[768]{0:T(1024)}, u32[]{:S(2)}) copy-start(f32[768]{0:T(1024)} %param.16) | copy-start | bytes 9220
  88.4 1.0 copy-start.10
  89.4 0.9 copy-start.12
  90.3 0.7 copy-start.18
  90.3 0.7 copy-start.20
  90.3 1.7 copy-start.22
  95.2 84.1 %copy-start.3 = (bf16[3,64,768]{2,1,0:T(8,128)(2,1)S(1)}, bf16[3,64,768]{2,1,0:T(8,128)(2,1)}, u32[]{:S(2)}) copy-start(bf16[3,64,768]{2,1,0:T(8,128)(2,1)} %reshape.99.mix_ref) | copy-start | bytes 884740
  179.3 1.7 copy-start
  187.6 1.4 copy-start.5
  189.0 0.8 copy-start.14
  190.5 11.6 %all-to-all-start = ((bf16[20,64,128]{2,1,0:T(8,128)(2,1)}), bf16[20,64,128]{2,1,0:T(8,128)(2,1)S(1)}, u32[]{:S(2)}, u32[]{:S(2)}) async-start(bf16[20,64,128]{2,1,0:T(8,128)(2,1)} %pad.4), calls=%async_computation | async-start | bytes 655360 | tf_op jit(solution)/shard_map/all_to_all | solution.py:933
  195.6 29.9 %collective-permute-start.1 = (bf16[3,16,768]{2,1,0:T(8,128)(2,1)}, bf16[3,16,768]{2,1,0:T(8,128)(2,1)S(1)}, u32[]{:S(2)}, u32[]{:S(2)}) collective-permute-start(bf16[3,16,768]{2,1,0:T(8,128)(2,1)} %get-tuple-element.112), channel_id=1, source_target_pairs={{1,0},{2,1},{3,2},{5,4},{6,5},{7,6},{9,8},{10,9},{11,10},{13,12},{... | collective-permute-start | bytes 221192 | tf_op jit(solution)/shard_map/ppermute | solution.py:907
  196.9 28.6 %collective-permute-start = (bf16[3,16,768]{2,1,0:T(8,128)(2,1)S(1)}, bf16[3,16,768]{2,1,0:T(8,128)(2,1)}, u32[]{:S(2)}, u32[]{:S(2)}) collective-permute-start(bf16[3,16,768]{2,1,0:T(8,128)(2,1)S(1)} %get-tuple-element.111), channel_id=1, source_target_pairs={{0,1},{1,2},{2,3},{4,5},{5,6},{6,7},{8,9},{9,10},{10,11},{12,13},{... | collective-permute-start | bytes 221192 | tf_op jit(solution)/shard_map/ppermute | solution.py:906
  202.2 1.2 copy-start.11
  203.4 1.1 copy-start.13
  204.4 0.9 copy-start.19
  205.4 0.9 copy-start.21
  206.3 0.9 copy-start.23
  218.9 0.7 copy-start.16
  219.6 31.1 %all-to-all-start.2 = ((f32[20,8,128]{2,1,0:T(8,128)}), f32[20,8,128]{2,1,0:T(8,128)S(1)}, u32[]{:S(2)}, u32[]{:S(2)}) async-start(f32[20,8,128]{2,1,0:T(8,128)} %bitcast.21), calls=%async_computation.2 | async-start | bytes 163840 | tf_op jit(solution)/shard_map/all_to_all | solution.py:960
  223.0 130.2 %reduce-scatter.19.cloned.1.call-start = ((), (), s32[]{:S(2)}) async-start(), calls=%async_computation.13 | async-start | bytes 1327104 | tf_op jit(solution)/shard_map/reduce_scatter | solution.py:912
  227.1 29.0 %copy-start.17 = (f32[5,64,128]{2,1,0:T(8,128)S(1)}, f32[5,64,128]{2,1,0:T(8,128)}, u32[]{:S(2)}) copy-start(f32[5,64,128]{2,1,0:T(8,128)} %copy-done.16) | copy-start | bytes 491524
  250.7 5.4 copy-start.15
  250.7 12.5 %all-to-all-start.1 = ((bf16[20,64,128]{2,1,0:T(8,128)(2,1)}), bf16[20,64,128]{2,1,0:T(8,128)(2,1)S(1)}, u32[]{:S(2)}, u32[]{:S(2)}) async-start(bf16[20,64,128]{2,1,0:T(8,128)(2,1)} %bitcast.20), calls=%async_computation.1 | async-start | bytes 655360 | tf_op jit(solution)/shard_map/all_to_all | solution.py:960
  256.0 114.5 %reduce-scatter.25.cloned.1.call-start = ((), (), s32[]{:S(2)}) async-start(), calls=%async_computation.17 | async-start | bytes 3981312
  269.3 14.9 %copy-start.6 = (bf16[3,512,768]{2,1,0:T(8,128)(2,1)}, bf16[3,512,768]{2,1,0:T(8,128)(2,1)S(1)}, u32[]{:S(2)}) copy-start(bf16[3,512,768]{2,1,0:T(8,128)(2,1)S(1)} %get-tuple-element.78.gv_ref) | copy-start | bytes 7077892
  269.3 14.9 %copy-start.7 = (bf16[3,512,768]{2,1,0:T(8,128)(2,1)}, bf16[3,512,768]{2,1,0:T(8,128)(2,1)S(1)}, u32[]{:S(2)}) copy-start(bf16[3,512,768]{2,1,0:T(8,128)(2,1)S(1)} %get-tuple-element.77.gk_ref) | copy-start | bytes 7077892
  323.2 105.1 %reduce-scatter.23.cloned.1.call-start = ((), (), s32[]{:S(2)}) async-start(), calls=%async_computation.15 | async-start | bytes 5308416 | tf_op jit(solution)/shard_map/reduce_scatter | solution.py:912
  338.2 147.4 %reduce-scatter.29.cloned.1.call-start = ((), (), s32[]{:S(2)}) async-start(), calls=%async_computation.19 | async-start | bytes 5308416
  351.5 0.8 copy-start.25
  351.5 0.9 copy-start.24
  351.5 139.7 %all-reduce.3.cloned.1.call-start = ((), (), s32[]{:S(2)}) async-start(), calls=%async_computation.16 | async-start | bytes 245760 | tf_op jit(solution)/shard_map/psum | solution.py:976
  353.1 154.6 %reduce-scatter.27.cloned.1.call-start = ((), (), s32[]{:S(2)}) async-start(), calls=%async_computation.18 | async-start | bytes 245760
  354.9 175.1 %reduce-scatter.17.cloned.1.call-start = ((), (), s32[]{:S(2)}) async-start(), calls=%async_computation.12 | async-start | bytes 737280 | tf_op jit(solution)/shard_map/reduce_scatter | solution.py:913
  372.6 180.2 %reduce-scatter.31.cloned.1.call-start = ((), (), s32[]{:S(2)}) async-start(), calls=%async_computation.20 | async-start | bytes 737280
  430.5 146.3 %reduce-scatter.21.cloned.1.call-start = ((), (), s32[]{:S(2)}) async-start(), calls=%async_computation.14 | async-start | bytes 983040 | tf_op jit(solution)/shard_map/reduce_scatter | solution.py:913
Sparse Core Ops, SparseCore 0:
  227.1 38.2 reduce-scatter.18
  323.3 47.1 reduce-scatter.24
  374.4 53.8 reduce-scatter.22
  431.6 53.9 reduce-scatter.28
  488.3 19.3 reduce-scatter.26
  509.9 20.1 reduce-scatter.16
  532.4 20.3 reduce-scatter.30
  555.1 21.6 reduce-scatter.20
Sparse Core Ops, SparseCore 1:
  358.1 133.0 all-reduce.2
